TPU v7x, 32 devices: a whole 2x2x4 slice. The times are simulated.
32 devices in a mesh: blk: 8 (over z, x), ulysses: 4 (over y, core).
Axes of the slice: x: 2, y: 2, z: 4, core: 2. Of those that a mesh axis runs over, the one named last changes fastest.
Arguments:
- tokens: bfloat16 [2, 2048, 768], P(None, ('blk', 'ulysses')), may hold values from -6 to 6
- attn_gain: bfloat16 [768], P(('blk', 'ulysses')), may hold values from 0.25 to 1.75
- qkv_weight: bfloat16 [768, 2304], P(('blk', 'ulysses')), may hold values from -0.3125 to 0.3125
- attn_out_weight: bfloat16 [768, 768], P(('blk', 'ulysses')), may hold values from -1.25 to 1.25
- mlp_gain: bfloat16 [768], P(('blk', 'ulysses')), may hold values from 0.25 to 1.75
- in_weight: bfloat16 [768, 2304], P(('blk', 'ulysses')), may hold values from -0.21875 to 0.21875
- out_weight: bfloat16 [1152, 768], P(None, ('blk', 'ulysses')), may hold values from -0.1875 to 0.1875
- cotangent: bfloat16 [2, 2048, 768], P(None, ('blk', 'ulysses')), may hold values from -6 to 6
Outputs:
- layer_output: bfloat16 [2, 2048, 768], P(None, ('blk', 'ulysses'))
- input_grad: bfloat16 [2, 2048, 768], P(None, ('blk', 'ulysses'))
- attn_gain_grad: float32 [768], P(('blk', 'ulysses'))
- qkv_weight_grad: float32 [768, 2304], P(('blk', 'ulysses'))
- attn_out_weight_grad: float32 [768, 768], P(('blk', 'ulysses'))
- mlp_gain_grad: float32 [768], P(('blk', 'ulysses'))
- in_weight_grad: float32 [768, 2304], P(('blk', 'ulysses'))
- out_weight_grad: float32 [1152, 768], P(None, ('blk', 'ulysses'))
All inputs are finite; a program needn't handle non-finite values.
Results may differ from a plain program's by a relative error of at most 0.018.
The roundings to bfloat16 on the way count: a program that leaves them out, or rounds other values in their place, can miss the bound.
Values may be sent and summed in bfloat16 or wider, within the bound.
No kernel may reach another device: no remote copies, remote signals or barrier semaphores. Data moves between devices by JAX's collectives and lax.ppermute only.
A program may use at most 256 MiB of HBM per device.

v0:
```python
import jax
import jax.numpy as jnp
from jax import lax
from jax.sharding import PartitionSpec as P

HEAD = 64
EPSILON = 1e-05
THETA = 160000.0


def from_behind(value, axis, by):
    size = lax.axis_size(axis)
    return lax.ppermute(value, axis, [(i, (i + by) % size) for i in range(size)])


def normalize(values):
    center = values - jnp.mean(values, axis=-1, keepdims=True)
    inverse = lax.rsqrt(jnp.mean(center * center, axis=-1, keepdims=True) + EPSILON)
    return (center * inverse, inverse)


def norm_back(grad_normed, normed, inverse):
    first_mean = jnp.mean(grad_normed, axis=-1, keepdims=True)
    second_mean = jnp.mean(grad_normed * normed, axis=-1, keepdims=True)
    return inverse * (grad_normed - first_mean - normed * second_mean)


def rotation(first_row, row_count, head_width):
    half_width = head_width // 2
    frequency = THETA ** (-(jnp.arange(half_width, dtype=jnp.float32) * 2.0) / head_width)
    positions = (first_row + jnp.arange(row_count, dtype=jnp.int32)).astype(jnp.float32)
    angles = positions[:, None] * frequency[None, :]
    cosine_table = jnp.concatenate([jnp.cos(angles), jnp.cos(angles)], axis=-1)
    sine_table = jnp.concatenate([jnp.sin(angles), jnp.sin(angles)], axis=-1)
    return (cosine_table, sine_table)


def rotate(values, cosine_table, sine_table, direction):
    half_width = values.shape[-1] // 2
    turned = jnp.concatenate([-values[..., half_width:], values[..., :half_width]], axis=-1)
    return values * cosine_table[:, None, :] + direction * turned * sine_table[:, None, :]


def block_grads(
    query_part,
    key_part,
    value_part,
    grad_part,
    log_part,
    dots_part,
    top_part,
    total_part,
    score_scale,
):
    scores = (
        jnp.einsum("sqhd,skhd->shqk", query_part, key_part, preferred_element_type=jnp.float32)
        * score_scale
    )
    probs = jnp.exp(scores - log_part[..., None])
    grad_probs = jnp.einsum(
        "sqhd,skhd->shqk", grad_part, value_part, preferred_element_type=jnp.float32
    )
    grad_scores = (probs * (grad_probs - dots_part[..., None])).astype(jnp.bfloat16)
    weights_low = jnp.exp(scores - top_part[..., None]).astype(jnp.bfloat16)
    grad_scaled = grad_part.astype(jnp.float32) / jnp.transpose(total_part, (0, 2, 1))[..., None]
    value_term = jnp.einsum("shqk,sqhd->skhd", weights_low.astype(jnp.float32), grad_scaled)
    return (value_term, grad_scores)


def body(
    tokens, attn_gain, qkv_weight, attn_out_weight, mlp_gain, in_weight, out_weight, cotangent
):
    sequences, per_device, model_width = tokens.shape
    groups = lax.axis_size("ulysses")
    cycle_size = lax.axis_size("blk")
    group_width = model_width // groups
    heads_here = group_width // HEAD
    group_rows = per_device * groups
    score_scale = HEAD ** (-0.5)
    qkv_full, attn_full, in_full, out_full, gain_one, gain_two = (
        lax.all_gather(qkv_weight, ("blk", "ulysses"), axis=0, tiled=True),
        lax.all_gather(attn_out_weight, ("blk", "ulysses"), axis=0, tiled=True),
        lax.all_gather(in_weight, ("blk", "ulysses"), axis=0, tiled=True),
        lax.all_gather(out_weight, ("blk", "ulysses"), axis=1, tiled=True),
        lax.all_gather(attn_gain, ("blk", "ulysses"), axis=0, tiled=True),
        lax.all_gather(mlp_gain, ("blk", "ulysses"), axis=0, tiled=True),
    )
    gain_one = gain_one.astype(jnp.float32)
    gain_two = gain_two.astype(jnp.float32)
    hidden_units = out_full.shape[0]
    inputs_wide = tokens.astype(jnp.float32).reshape(sequences * per_device, model_width)
    normed_one, inverse_one = normalize(inputs_wide)
    hidden_one = (normed_one * gain_one).astype(jnp.bfloat16)
    qkv = jnp.dot(hidden_one, qkv_full, preferred_element_type=jnp.float32).astype(jnp.bfloat16)
    packed = qkv.reshape(sequences, per_device, 3, groups, group_width)
    headwise = lax.all_to_all(packed, "ulysses", split_axis=3, concat_axis=1, tiled=True)
    headwise = headwise.reshape(sequences, group_rows, 3, heads_here, HEAD)
    cosine_table, sine_table = rotation(lax.axis_index("blk") * group_rows, group_rows, HEAD)
    queries = rotate(headwise[:, :, 0].astype(jnp.float32), cosine_table, sine_table, 1.0).astype(
        jnp.bfloat16
    )
    key_rows = rotate(headwise[:, :, 1].astype(jnp.float32), cosine_table, sine_table, 1.0).astype(
        jnp.bfloat16
    )
    value_rows = headwise[:, :, 2]
    start_top = jnp.full((sequences, heads_here, group_rows), -1e30, jnp.float32)
    zeros_rows = jnp.zeros((sequences, group_rows, heads_here, HEAD), jnp.float32)
    key_piece = lax.all_gather(key_rows, "blk", axis=1, tiled=True)
    value_piece = lax.all_gather(value_rows, "blk", axis=1, tiled=True)
    scores = (
        jnp.einsum("sqhd,skhd->shqk", queries, key_piece, preferred_element_type=jnp.float32)
        * score_scale
    )
    new_top = jnp.maximum(start_top, jnp.max(scores, axis=-1))
    weights = jnp.exp(scores - new_top[..., None])
    attend_row_total = jnp.sum(weights, axis=-1)
    update = jnp.einsum(
        "shqk,skhd->sqhd",
        weights.astype(jnp.bfloat16),
        value_piece,
        preferred_element_type=jnp.float32,
    )
    weighted = update
    row_top, row_total, weighted = (new_top, attend_row_total, weighted)
    log_total = row_top + jnp.log(row_total)
    attn_wide = weighted / jnp.transpose(row_total, (0, 2, 1))[..., None]
    attn_low = attn_wide.astype(jnp.bfloat16).reshape(sequences, group_rows, 1, group_width)
    token_rows = lax.all_to_all(attn_low, "ulysses", split_axis=1, concat_axis=2, tiled=True)
    attn_cat = token_rows.reshape(sequences * per_device, model_width)
    middle = inputs_wide + jnp.dot(attn_cat, attn_full, preferred_element_type=jnp.float32)
    normed_two, inverse_two = normalize(middle)
    hidden_two = (normed_two * gain_two).astype(jnp.bfloat16)
    joint = jnp.dot(hidden_two, in_full, preferred_element_type=jnp.float32)

    def geglu(joint_pre):
        return (
            jax.nn.gelu(joint_pre[:, :hidden_units], approximate=False)
            * joint_pre[:, hidden_units:]
        )

    act_wide, geglu_back = jax.vjp(geglu, joint)
    activation = act_wide.astype(jnp.bfloat16)
    result = middle + jnp.dot(activation, out_full, preferred_element_type=jnp.float32)
    layer_output = result.astype(jnp.bfloat16).reshape(sequences, per_device, model_width)
    grad_out = cotangent.reshape(sequences * per_device, model_width)
    grad_wout = jnp.einsum("tf,td->fd", activation, grad_out, preferred_element_type=jnp.float32)
    grad_act = jnp.einsum("td,fd->tf", grad_out, out_full, preferred_element_type=jnp.float32)
    grad_joint = geglu_back(grad_act)[0].astype(jnp.bfloat16)
    grad_win = jnp.einsum("tc,tf->cf", hidden_two, grad_joint, preferred_element_type=jnp.float32)
    grad_hidden_two = jnp.einsum(
        "tf,cf->tc", grad_joint, in_full, preferred_element_type=jnp.float32
    )
    grad_gain_two = jnp.sum(grad_hidden_two * normed_two, axis=0)
    grad_middle = grad_out.astype(jnp.float32) + norm_back(
        grad_hidden_two * gain_two, normed_two, inverse_two
    )
    grad_branch = grad_middle.astype(jnp.bfloat16)
    grad_wattn = jnp.einsum("tc,td->cd", attn_cat, grad_branch, preferred_element_type=jnp.float32)
    grad_cat = jnp.einsum(
        "td,cd->tc", grad_branch, attn_full, preferred_element_type=jnp.float32
    ).astype(jnp.bfloat16)
    grad_heads_in = lax.all_to_all(
        grad_cat.reshape(sequences, per_device, groups, group_width),
        "ulysses",
        split_axis=2,
        concat_axis=1,
        tiled=True,
    )
    grad_attn = grad_heads_in.reshape(sequences, group_rows, heads_here, HEAD)
    row_dots = jnp.transpose(jnp.sum(grad_attn.astype(jnp.float32) * attn_wide, axis=-1), (0, 2, 1))

    def cycle_step(step_index, state_now):
        key_now, value_now, grad_key, grad_value, grad_query = state_now
        value_term, grad_scores = block_grads(
            queries,
            key_now,
            value_now,
            grad_attn,
            log_total,
            row_dots,
            row_top,
            row_total,
            score_scale,
        )
        grad_value = grad_value + value_term
        grad_key = grad_key + score_scale * jnp.einsum(
            "shqk,sqhd->skhd", grad_scores, queries, preferred_element_type=jnp.float32
        )
        grad_query = grad_query + score_scale * jnp.einsum(
            "shqk,skhd->sqhd", grad_scores, key_now, preferred_element_type=jnp.float32
        )
        key_now, value_now = from_behind((key_now, value_now), "blk", 1)
        grad_key, grad_value = (
            from_behind(grad_key.astype(jnp.bfloat16), "blk", 1).astype(grad_key.dtype),
            from_behind(grad_value.astype(jnp.bfloat16), "blk", 1).astype(grad_value.dtype),
        )
        return (key_now, value_now, grad_key, grad_value, grad_query)

    final_state = lax.fori_loop(
        0, cycle_size, cycle_step, (key_rows, value_rows, zeros_rows, zeros_rows, zeros_rows)
    )
    grad_key, grad_value, grad_query = (final_state[2], final_state[3], final_state[4])
    grad_query = rotate(grad_query, cosine_table, sine_table, -1.0)
    grad_key = rotate(grad_key, cosine_table, sine_table, -1.0)
    grad_stack = jnp.stack([grad_query, grad_key, grad_value], axis=2).astype(jnp.bfloat16)
    grad_stack = grad_stack.reshape(sequences, group_rows, 3, 1, group_width)
    grad_tokens = lax.all_to_all(grad_stack, "ulysses", split_axis=1, concat_axis=3, tiled=True)
    grad_qkv = grad_tokens.reshape(sequences * per_device, 3 * model_width)
    grad_wqkv = jnp.einsum("tc,tf->cf", hidden_one, grad_qkv, preferred_element_type=jnp.float32)
    grad_hidden_one = jnp.einsum(
        "tf,cf->tc", grad_qkv, qkv_full, preferred_element_type=jnp.float32
    )
    grad_gain_one = jnp.sum(grad_hidden_one * normed_one, axis=0)
    grad_input = grad_middle + norm_back(grad_hidden_one * gain_one, normed_one, inverse_one)
    input_grad = grad_input.astype(jnp.bfloat16).reshape(sequences, per_device, model_width)
    shard_qkv, shard_attn, shard_in, shard_out, shard_one, shard_two = (
        lax.psum_scatter(grad_wqkv, ("blk", "ulysses"), scatter_dimension=0, tiled=True),
        lax.psum_scatter(grad_wattn, ("blk", "ulysses"), scatter_dimension=0, tiled=True),
        lax.psum_scatter(grad_win, ("blk", "ulysses"), scatter_dimension=0, tiled=True),
        lax.psum_scatter(grad_wout, ("blk", "ulysses"), scatter_dimension=1, tiled=True),
        lax.psum_scatter(grad_gain_one, ("blk", "ulysses"), scatter_dimension=0, tiled=True),
        lax.psum_scatter(grad_gain_two, ("blk", "ulysses"), scatter_dimension=0, tiled=True),
    )
    return (
        layer_output,
        input_grad,
        shard_one,
        shard_qkv,
        shard_attn,
        shard_two,
        shard_in,
        shard_out,
    )


def solution(mesh):
    placed = (
        P(None, ("blk", "ulysses"), None),
        P(("blk", "ulysses")),
        P(("blk", "ulysses"), None),
        P(("blk", "ulysses"), None),
        P(("blk", "ulysses")),
        P(("blk", "ulysses"), None),
        P(None, ("blk", "ulysses")),
        P(None, ("blk", "ulysses"), None),
    )
    return jax.shard_map(
        body,
        mesh=mesh,
        in_specs=placed,
        out_specs=(
            P(None, ("blk", "ulysses"), None),
            P(None, ("blk", "ulysses"), None),
            P(("blk", "ulysses")),
            P(("blk", "ulysses"), None),
            P(("blk", "ulysses"), None),
            P(("blk", "ulysses")),
            P(("blk", "ulysses"), None),
            P(None, ("blk", "ulysses")),
        ),
        check_vma=False,
    )
```

profile of v0, /device:TPU:0, one launch (start us, length us, event | category | flops | bytes accessed | tf_op | source)
XLA Modules:
  0.0 867.9 jit_solution(4147596167485549714)
XLA Ops:
  9.6 42.2 %all-reduce.8 = (bf16[768]{0:T(1024)(128)(2,1)S(1)}, bf16[768]{0:T(1024)(128)(2,1)S(1)}) all-reduce(bf16[768]{0:T(1024)(128)(2,1)S(1)} %dynamic-update-slice, bf16[768]{0:T(1024)(128)(2,1)S(1)} %dynamic-update-slice.1), channel_id=1, replica_groups=mesh['blk'=8,'ulysses'=4] {'blk','ulysses'}, use_global_device_ids=true, to_apply=%add.2 | all-reduce | flops 1536 | bytes 6144
  55.8 18.1 %all-gather.8.cloned.1.call-done = bf16[768,2304]{1,0:T(8,128)(2,1)} async-done(((bf16[24,2304]{1,0:T(8,128)(2,1)}), bf16[768,2304]{1,0:T(8,128)(2,1)}) %all-gather.8.cloned.1.call-update) | async-done | bytes 3538960 | tf_op jit(solution)/shard_map/all_gather | solution.py:81
  73.8 2.6 convolution_convert_fusion
  78.3 3.5 all-to-all-start
  82.7 10.7 %all-to-all-done = bf16[2,64,3,4,192]{4,1,2,0,3:T(8,128)(2,1)S(1)} async-done(((bf16[2,64,3,4,192]{4,1,2,0,3:T(8,128)(2,1)}), bf16[2,64,3,4,192]{4,1,2,0,3:T(8,128)(2,1)S(1)}, u32[]{:S(2)}, u32[]{:S(2)}) %all-to-all-start) | async-done | bytes 589856 | tf_op jit(solution)/shard_map/all_to_all | solution.py:96
  99.1 41.7 %all-gather.10.cloned.1.call-done = bf16[2,2048,3,64]{1,3,2,0:T(8,128)(2,1)} async-done(((bf16[2,256,3,64]{1,3,2,0:T(8,128)(2,1)}), bf16[2,2048,3,64]{1,3,2,0:T(8,128)(2,1)}) %all-gather.10.cloned.1.call-update) | async-done | bytes 1572880 | tf_op jit(solution)/shard_map/all_gather | solution.py:108
  140.8 3.3 multiply_reduce_fusion
  144.2 4.5 copy-done
  148.6 2.4 fusion.11
  151.1 35.8 %all-gather.18.cloned.1.call-done = bf16[2,2048,1,3,64]{1,4,3,0,2:T(8,128)(2,1)} async-done(((bf16[2,256,1,3,64]{1,4,3,0,2:T(8,128)(2,1)}), bf16[2,2048,1,3,64]{1,4,3,0,2:T(8,128)(2,1)}) %all-gather.18.cloned.1.call-update) | async-done | bytes 1572880 | tf_op jit(solution)/shard_map/all_gather | solution.py:109
  186.9 8.2 fusion.56
  196.0 3.4 all-to-all-start.1
  199.6 5.8 all-to-all-done.1
  205.9 36.1 %all-gather.12.cloned.1.call-done = bf16[768,768]{1,0:T(8,128)(2,1)} async-done(((bf16[24,768]{1,0:T(8,128)(2,1)}), bf16[768,768]{1,0:T(8,128)(2,1)}) %all-gather.12.cloned.1.call-update) | async-done | bytes 1179664 | tf_op jit(solution)/shard_map/all_gather | solution.py:82
  244.0 59.9 %all-gather.14.cloned.1.call-done = bf16[768,2304]{1,0:T(8,128)(2,1)} async-done(((bf16[24,2304]{1,0:T(8,128)(2,1)}), bf16[768,2304]{1,0:T(8,128)(2,1)}) %all-gather.14.cloned.1.call-update) | async-done | bytes 3538960 | tf_op jit(solution)/shard_map/all_gather | solution.py:83
  303.9 2.7 fusion.54
  306.6 54.5 %all-gather.16.cloned.1.call-done = bf16[1152,768]{0,1:T(8,128)(2,1)} async-done(((bf16[1152,24]{0,1:T(8,128)(2,1)}), bf16[1152,768]{0,1:T(8,128)(2,1)}) %all-gather.16.cloned.1.call-update) | async-done | bytes 1769488 | tf_op jit(solution)/shard_map/all_gather | solution.py:84
  361.1 3.2 fusion.45
  364.6 1.9 multiply_reduce_fusion.1
  366.8 1.9 fusion.46
  368.8 2.5 fusion.59
  375.7 3.4 all-to-all-start.2
  379.2 4.7 fusion.49
  387.3 184.9 %while.19 = (s32[]{:T(128)}, bf16[2,256,3,64]{1,3,2,0:T(8,128)(2,1)}, bf16[2,256,3,64]{1,3,2,0:T(8,128)(2,1)}, f32[2,256,3,64]{1,3,2,0:T(8,128)}, f32[2,256,3,64...) while((s32[]{:T(128)}, ...), condition=%wide.region_10.0_spmd.clone, body=%wide.region_9.0_spmd.clone.sunk | while | flops 255787008 | bytes 18751904 | solution.py:199
  395.6 2.0 fusion.110
  399.7 7.6 collective-permute-done.2
  407.3 1.7 convert_element_type.208
  416.4 2.0 fusion.110
  418.5 1.8 collective-permute-start.3
  420.3 2.1 fusion.111
  422.4 14.6 %collective-permute-done.2 = bf16[2,256,3,64]{1,3,2,0:T(8,128)(2,1)} collective-permute-done((bf16[2,256,3,64]{1,3,2,0:T(8,128)(2,1)}, bf16[2,256,3,64]{1,3,2,0:T(8,128)(2,1)}, u32[]{:S(2)}, u32[]{:S(2)}) %collective-permute-start.2) | collective-permute-done | bytes 196640 | tf_op jit(solution)/shard_map/while/body/eval_jaxpr/ppermute | solution.py:13
  437.0 1.7 convert_element_type.208
  444.8 2.0 fusion.110
  447.0 2.1 fusion.111
  449.1 12.9 %collective-permute-done.2 = bf16[2,256,3,64]{1,3,2,0:T(8,128)(2,1)} collective-permute-done((bf16[2,256,3,64]{1,3,2,0:T(8,128)(2,1)}, bf16[2,256,3,64]{1,3,2,0:T(8,128)(2,1)}, u32[]{:S(2)}, u32[]{:S(2)}) %collective-permute-start.2) | collective-permute-done | bytes 196640 | tf_op jit(solution)/shard_map/while/body/eval_jaxpr/ppermute | solution.py:13
  462.1 1.7 convert_element_type.208
  469.8 2.0 fusion.110
  471.9 2.2 fusion.111
  474.0 10.6 %collective-permute-done.2 = bf16[2,256,3,64]{1,3,2,0:T(8,128)(2,1)} collective-permute-done((bf16[2,256,3,64]{1,3,2,0:T(8,128)(2,1)}, bf16[2,256,3,64]{1,3,2,0:T(8,128)(2,1)}, u32[]{:S(2)}, u32[]{:S(2)}) %collective-permute-start.2) | collective-permute-done | bytes 196640 | tf_op jit(solution)/shard_map/while/body/eval_jaxpr/ppermute | solution.py:13
  492.4 2.0 fusion.110
  494.5 2.2 fusion.111
  496.6 8.0 collective-permute-done.2
  504.6 1.7 convert_element_type.208
  512.4 2.0 fusion.110
  514.4 2.9 collective-permute-start.3
  517.4 2.2 fusion.111
  519.6 4.2 collective-permute-done.2
  523.8 1.7 convert_element_type.208
  528.5 2.8 collective-permute-start.1
  534.4 2.0 fusion.110
  537.0 2.2 fusion.111
  539.1 3.9 collective-permute-done.2
  552.3 2.0 fusion.110
  554.4 1.9 collective-permute-start.3
  556.3 2.2 fusion.111
  558.5 11.0 %collective-permute-done.2 = bf16[2,256,3,64]{1,3,2,0:T(8,128)(2,1)} collective-permute-done((bf16[2,256,3,64]{1,3,2,0:T(8,128)(2,1)}, bf16[2,256,3,64]{1,3,2,0:T(8,128)(2,1)}, u32[]{:S(2)}, u32[]{:S(2)}) %collective-permute-start.2) | collective-permute-done | bytes 196640 | tf_op jit(solution)/shard_map/while/body/eval_jaxpr/ppermute | solution.py:13
  575.8 1.8 copy.48
  577.6 5.3 all-to-all-start.3
  583.1 11.5 %all-to-all-done.3 = bf16[2,256,3,1,192]{4,0,3,2,1:T(2,128)(2,1)S(1)} async-done(((bf16[2,256,3,1,192]{4,0,3,2,1:T(2,128)(2,1)}), bf16[2,256,3,1,192]{4,0,3,2,1:T(2,128)(2,1)S(1)}, u32[]{:S(2)}, u32[]{:S(2)}) %all-to-all-start.3) | async-done | bytes 589856 | tf_op jit(solution)/shard_map/all_to_all | solution.py:207
  596.0 4.0 fusion.58
  603.0 3.5 multiply_reduce_fusion.2
  606.4 37.0 %all-reduce.7 = (f32[768]{0:T(1024)S(1)}, f32[768]{0:T(1024)S(1)}) all-reduce(f32[768]{0:T(1024)S(1)} %get-tuple-element.116, f32[768]{0:T(1024)S(1)} %copy-done.28), channel_id=3, replica_groups=mesh['blk'=8,'ulysses'=4] {'blk','ulysses'}, use_global_device_ids=true, to_apply=%region_14.0.clone | all-reduce | flops 1536 | bytes 12288
  645.5 91.0 %reduce-scatter.11.cloned.1.call-done = f32[24,2304]{1,0:T(8,128)} async-done(((f32[768,2304]{1,0:T(8,128)}), f32[24,2304]{1,0:T(8,128)}) %reduce-scatter.11.cloned.1.call-update) | async-done | bytes 221200 | tf_op jit(solution)/shard_map/reduce_scatter | solution.py:219
  736.5 124.6 %reduce-scatter.7.cloned.1.call-done = f32[24,2304]{1,0:T(8,128)} async-done(((f32[768,2304]{1,0:T(8,128)}), f32[24,2304]{1,0:T(8,128)}) %reduce-scatter.7.cloned.1.call-update) | async-done | bytes 221200 | tf_op jit(solution)/shard_map/reduce_scatter | solution.py:217
  (321 shorter events, 98.6 us)
Async XLA Ops:
  7.2 66.7 %all-gather.8.cloned.1.call-start = ((), (), s32[]{:S(2)}) async-start(), calls=%async_computation.8 | async-start | bytes 3649536 | tf_op jit(solution)/shard_map/all_gather | solution.py:81
  51.8 22.0 %copy-start.21 = (f32[768]{0:T(1024)}, f32[768]{0:T(1024)S(1)}, u32[]{:S(2)}) copy-start(f32[768]{0:T(1024)S(1)} %convert_element_type.109) | copy-start | bytes 9220
  52.9 20.9 %copy-start.32 = (f32[128]{0:T(128)}, f32[128]{0:T(128)S(1)}, u32[]{:S(2)}) copy-start(f32[128]{0:T(128)S(1)} %div.49) | copy-start | bytes 1540
  54.2 19.7 %copy-start.34 = (f32[128]{0:T(128)}, f32[128]{0:T(128)S(1)}, u32[]{:S(2)}) copy-start(f32[128]{0:T(128)S(1)} %rsqrt.21) | copy-start | bytes 1540
  78.3 15.1 %all-to-all-start = ((bf16[2,64,3,4,192]{4,1,2,0,3:T(8,128)(2,1)}), bf16[2,64,3,4,192]{4,1,2,0,3:T(8,128)(2,1)S(1)}, u32[]{:S(2)}, u32[]{:S(2)}) async-start(bf16[2,64,3,4,192]{4,1,2,0,3:T(8,128)(2,1)} %copy.38), calls=%async_computation | async-start | bytes 1572864 | tf_op jit(solution)/shard_map/all_to_all | solution.py:96
  81.8 59.0 %all-gather.10.cloned.1.call-start = ((), (), s32[]{:S(2)}) async-start(), calls=%async_computation.9 | async-start | bytes 1769472 | tf_op jit(solution)/shard_map/all_gather | solution.py:108
  82.0 13.7 %copy-start.17 = (f32[256,64]{0,1:T(8,128)}, f32[256,64]{0,1:T(8,128)S(1)}, u32[]{:S(2)}) copy-start(f32[256,64]{0,1:T(8,128)S(1)} %pad_maximum_fusion.1) | copy-start | bytes 196612
  96.6 90.3 %all-gather.18.cloned.1.call-start = ((), (), s32[]{:S(2)}) async-start(), calls=%async_computation.16 | async-start | bytes 1769472 | tf_op jit(solution)/shard_map/all_gather | solution.py:109
  97.3 144.7 %all-gather.12.cloned.1.call-start = ((), (), s32[]{:S(2)}) async-start(), calls=%async_computation.10 | async-start | bytes 1216512 | tf_op jit(solution)/shard_map/all_gather | solution.py:82
  97.9 206.0 %all-gather.14.cloned.1.call-start = ((), (), s32[]{:S(2)}) async-start(), calls=%async_computation.11 | async-start | bytes 3649536 | tf_op jit(solution)/shard_map/all_gather | solution.py:83
  98.5 262.6 %all-gather.16.cloned.1.call-start = ((), (), s32[]{:S(2)}) async-start(), calls=%async_computation.12 | async-start | bytes 1824768 | tf_op jit(solution)/shard_map/all_gather | solution.py:84
  144.1 4.5 copy-start
  144.1 7.0 copy-start.27
  144.1 42.8 %copy-start.25 = (f32[2,3,256]{2,1,0:T(4,128)}, f32[2,3,256]{2,1,0:T(4,128)S(1)}, u32[]{:S(2)}) copy-start(f32[2,3,256]{2,1,0:T(4,128)S(1)} %broadcast_maximum_fusion) | copy-start | bytes 18436
  151.1 44.0 %copy-start.23 = (f32[2,3,256]{2,1,0:T(4,128)}, f32[2,3,256]{2,1,0:T(4,128)S(1)}, u32[]{:S(2)}) copy-start(f32[2,3,256]{2,1,0:T(4,128)S(1)} %fusion.11) | copy-start | bytes 18436
  195.1 46.9 %copy-start.5 = (bf16[2,64,768]{2,1,0:T(8,128)(2,1)S(1)}, bf16[2,64,768]{2,1,0:T(8,128)(2,1)}, u32[]{:S(2)}) copy-start(bf16[2,64,768]{2,1,0:T(8,128)(2,1)} %param.10) | copy-start | bytes 589828
  196.0 9.4 %all-to-all-start.1 = ((bf16[2,256,1,192]{3,0,2,1:T(2,128)(2,1)}), bf16[2,256,1,192]{3,0,2,1:T(2,128)(2,1)S(1)}, u32[]{:S(2)}, u32[]{:S(2)}) async-start(bf16[2,256,1,192]{3,0,2,1:T(2,128)(2,1)} %copy.43), calls=%async_computation.1 | async-start | bytes 524288 | tf_op jit(solution)/shard_map/all_to_all | solution.py:128
  199.4 446.1 %reduce-scatter.9.cloned.1.call-start = ((), (), s32[]{:S(2)}) async-start(), calls=%async_computation.14 | async-start | bytes 2433024 | tf_op jit(solution)/shard_map/reduce_scatter | solution.py:218
  243.9 122.6 %copy-start.29 = (f32[128]{0:T(128)}, f32[128]{0:T(128)S(1)}, u32[]{:S(2)}) copy-start(f32[128]{0:T(128)S(1)} %add_rsqrt_fusion.1) | copy-start | bytes 1540
  243.9 117.1 %copy-start.15 = (bf16[2,64,768]{2,1,0:T(8,128)(2,1)S(1)}, bf16[2,64,768]{2,1,0:T(8,128)(2,1)}, u32[]{:S(2)}) copy-start(bf16[2,64,768]{2,1,0:T(8,128)(2,1)} %param.17) | copy-start | bytes 589828
  364.6 4.2 copy-start.9
  366.8 5.4 copy-start.6
  368.7 276.7 %reduce-scatter.13.cloned.1.call-start = ((), (), s32[]{:S(2)}) async-start(), calls=%async_computation.17 | async-start | bytes 3649536
  371.3 7.9 copy-start.12
  375.7 9.4 %all-to-all-start.2 = ((bf16[2,64,4,192]{3,1,0,2:T(8,128)(2,1)}), bf16[2,64,4,192]{3,1,0,2:T(8,128)(2,1)S(1)}, u32[]{:S(2)}, u32[]{:S(2)}) async-start(bf16[2,64,4,192]{3,1,0,2:T(8,128)(2,1)} %copy.46), calls=%async_computation.2 | async-start | bytes 524288 | tf_op jit(solution)/shard_map/all_to_all | solution.py:162
  379.1 357.4 %reduce-scatter.11.cloned.1.call-start = ((), (), s32[]{:S(2)}) async-start(), calls=%async_computation.15 | async-start | bytes 7299072 | tf_op jit(solution)/shard_map/reduce_scatter | solution.py:219
  388.3 22.6 %collective-permute-start = (bf16[2,256,3,64]{1,3,2,0:T(8,128)(2,1)S(1)}, bf16[2,256,3,64]{1,3,2,0:T(8,128)(2,1)}, u32[]{:S(2)}, u32[]{:S(2)}) collective-permute-start(bf16[2,256,3,64]{1,3,2,0:T(8,128)(2,1)S(1)} %copy.62), channel_id=1, source_target_pairs={{0,4},{4,8},{8,12},{12,16},{16,20},{20,24},{24,28},{28,0},{1,5},{5... | collective-permute-start | bytes 589832 | tf_op jit(solution)/shard_map/while/body/eval_jaxpr/ppermute | solution.py:13
  390.6 20.3 %collective-permute-start.1 = (bf16[2,256,3,64]{1,3,2,0:T(8,128)(2,1)S(1)}, bf16[2,256,3,64]{1,3,2,0:T(8,128)(2,1)}, u32[]{:S(2)}, u32[]{:S(2)}) collective-permute-start(bf16[2,256,3,64]{1,3,2,0:T(8,128)(2,1)S(1)} %copy.63), channel_id=1, source_target_pairs={{0,4},{4,8},{8,12},{12,16},{16,20},{20,24},{24,28},{28,0},{1,5},{5... | collective-permute-start | bytes 589832 | tf_op jit(solution)/shard_map/while/body/eval_jaxpr/ppermute | solution.py:13
  394.2 13.1 %collective-permute-start.2 = (bf16[2,256,3,64]{1,3,2,0:T(8,128)(2,1)}, bf16[2,256,3,64]{1,3,2,0:T(8,128)(2,1)}, u32[]{:S(2)}, u32[]{:S(2)}) collective-permute-start(bf16[2,256,3,64]{1,3,2,0:T(8,128)(2,1)} %fusion.109), channel_id=1, source_target_pairs={{0,4},{4,8},{8,12},{12,16},{16,20},{20,24},{24,28},{28,0},{1,5},{5... | collective-permute-start | bytes 589832 | tf_op jit(solution)/shard_map/while/body/eval_jaxpr/ppermute | solution.py:13
  397.6 12.4 %collective-permute-start.3 = (bf16[2,256,3,64]{1,3,2,0:T(8,128)(2,1)}, bf16[2,256,3,64]{1,3,2,0:T(8,128)(2,1)S(1)}, u32[]{:S(2)}, u32[]{:S(2)}) collective-permute-start(bf16[2,256,3,64]{1,3,2,0:T(8,128)(2,1)} %fusion.110), channel_id=1, source_target_pairs={{0,4},{4,8},{8,12},{12,16},{16,20},{20,24},{24,28},{28,0},{1,5},{5... | collective-permute-start | bytes 589832 | tf_op jit(solution)/shard_map/while/body/eval_jaxpr/ppermute | solution.py:13
  411.8 28.1 %collective-permute-start = (bf16[2,256,3,64]{1,3,2,0:T(8,128)(2,1)S(1)}, bf16[2,256,3,64]{1,3,2,0:T(8,128)(2,1)}, u32[]{:S(2)}, u32[]{:S(2)}) collective-permute-start(bf16[2,256,3,64]{1,3,2,0:T(8,128)(2,1)S(1)} %copy.62), channel_id=1, source_target_pairs={{0,4},{4,8},{8,12},{12,16},{16,20},{20,24},{24,28},{28,0},{1,5},{5... | collective-permute-start | bytes 589832 | tf_op jit(solution)/shard_map/while/body/eval_jaxpr/ppermute | solution.py:13
  412.7 27.1 %collective-permute-start.1 = (bf16[2,256,3,64]{1,3,2,0:T(8,128)(2,1)S(1)}, bf16[2,256,3,64]{1,3,2,0:T(8,128)(2,1)}, u32[]{:S(2)}, u32[]{:S(2)}) collective-permute-start(bf16[2,256,3,64]{1,3,2,0:T(8,128)(2,1)S(1)} %copy.63), channel_id=1, source_target_pairs={{0,4},{4,8},{8,12},{12,16},{16,20},{20,24},{24,28},{28,0},{1,5},{5... | collective-permute-start | bytes 589832 | tf_op jit(solution)/shard_map/while/body/eval_jaxpr/ppermute | solution.py:13
  415.9 21.1 %collective-permute-start.2 = (bf16[2,256,3,64]{1,3,2,0:T(8,128)(2,1)}, bf16[2,256,3,64]{1,3,2,0:T(8,128)(2,1)}, u32[]{:S(2)}, u32[]{:S(2)}) collective-permute-start(bf16[2,256,3,64]{1,3,2,0:T(8,128)(2,1)} %fusion.109), channel_id=1, source_target_pairs={{0,4},{4,8},{8,12},{12,16},{16,20},{20,24},{24,28},{28,0},{1,5},{5... | collective-permute-start | bytes 589832 | tf_op jit(solution)/shard_map/while/body/eval_jaxpr/ppermute | solution.py:13
  418.5 20.6 %collective-permute-start.3 = (bf16[2,256,3,64]{1,3,2,0:T(8,128)(2,1)}, bf16[2,256,3,64]{1,3,2,0:T(8,128)(2,1)S(1)}, u32[]{:S(2)}, u32[]{:S(2)}) collective-permute-start(bf16[2,256,3,64]{1,3,2,0:T(8,128)(2,1)} %fusion.110), channel_id=1, source_target_pairs={{0,4},{4,8},{8,12},{12,16},{16,20},{20,24},{24,28},{28,0},{1,5},{5... | collective-permute-start | bytes 589832 | tf_op jit(solution)/shard_map/while/body/eval_jaxpr/ppermute | solution.py:13
  440.8 24.1 %collective-permute-start = (bf16[2,256,3,64]{1,3,2,0:T(8,128)(2,1)S(1)}, bf16[2,256,3,64]{1,3,2,0:T(8,128)(2,1)}, u32[]{:S(2)}, u32[]{:S(2)}) collective-permute-start(bf16[2,256,3,64]{1,3,2,0:T(8,128)(2,1)S(1)} %copy.62), channel_id=1, source_target_pairs={{0,4},{4,8},{8,12},{12,16},{16,20},{20,24},{24,28},{28,0},{1,5},{5... | collective-permute-start | bytes 589832 | tf_op jit(solution)/shard_map/while/body/eval_jaxpr/ppermute | solution.py:13
  441.7 23.2 %collective-permute-start.1 = (bf16[2,256,3,64]{1,3,2,0:T(8,128)(2,1)S(1)}, bf16[2,256,3,64]{1,3,2,0:T(8,128)(2,1)}, u32[]{:S(2)}, u32[]{:S(2)}) collective-permute-start(bf16[2,256,3,64]{1,3,2,0:T(8,128)(2,1)S(1)} %copy.63), channel_id=1, source_target_pairs={{0,4},{4,8},{8,12},{12,16},{16,20},{20,24},{24,28},{28,0},{1,5},{5... | collective-permute-start | bytes 589832 | tf_op jit(solution)/shard_map/while/body/eval_jaxpr/ppermute | solution.py:13
  444.8 17.3 %collective-permute-start.2 = (bf16[2,256,3,64]{1,3,2,0:T(8,128)(2,1)}, bf16[2,256,3,64]{1,3,2,0:T(8,128)(2,1)}, u32[]{:S(2)}, u32[]{:S(2)}) collective-permute-start(bf16[2,256,3,64]{1,3,2,0:T(8,128)(2,1)} %fusion.109), channel_id=1, source_target_pairs={{0,4},{4,8},{8,12},{12,16},{16,20},{20,24},{24,28},{28,0},{1,5},{5... | collective-permute-start | bytes 589832 | tf_op jit(solution)/shard_map/while/body/eval_jaxpr/ppermute | solution.py:13
  446.8 17.2 %collective-permute-start.3 = (bf16[2,256,3,64]{1,3,2,0:T(8,128)(2,1)}, bf16[2,256,3,64]{1,3,2,0:T(8,128)(2,1)S(1)}, u32[]{:S(2)}, u32[]{:S(2)}) collective-permute-start(bf16[2,256,3,64]{1,3,2,0:T(8,128)(2,1)} %fusion.110), channel_id=1, source_target_pairs={{0,4},{4,8},{8,12},{12,16},{16,20},{20,24},{24,28},{28,0},{1,5},{5... | collective-permute-start | bytes 589832 | tf_op jit(solution)/shard_map/while/body/eval_jaxpr/ppermute | solution.py:13
  465.8 21.6 %collective-permute-start = (bf16[2,256,3,64]{1,3,2,0:T(8,128)(2,1)S(1)}, bf16[2,256,3,64]{1,3,2,0:T(8,128)(2,1)}, u32[]{:S(2)}, u32[]{:S(2)}) collective-permute-start(bf16[2,256,3,64]{1,3,2,0:T(8,128)(2,1)S(1)} %copy.62), channel_id=1, source_target_pairs={{0,4},{4,8},{8,12},{12,16},{16,20},{20,24},{24,28},{28,0},{1,5},{5... | collective-permute-start | bytes 589832 | tf_op jit(solution)/shard_map/while/body/eval_jaxpr/ppermute | solution.py:13
  466.7 20.7 %collective-permute-start.1 = (bf16[2,256,3,64]{1,3,2,0:T(8,128)(2,1)S(1)}, bf16[2,256,3,64]{1,3,2,0:T(8,128)(2,1)}, u32[]{:S(2)}, u32[]{:S(2)}) collective-permute-start(bf16[2,256,3,64]{1,3,2,0:T(8,128)(2,1)S(1)} %copy.63), channel_id=1, source_target_pairs={{0,4},{4,8},{8,12},{12,16},{16,20},{20,24},{24,28},{28,0},{1,5},{5... | collective-permute-start | bytes 589832 | tf_op jit(solution)/shard_map/while/body/eval_jaxpr/ppermute | solution.py:13
  469.8 14.8 %collective-permute-start.2 = (bf16[2,256,3,64]{1,3,2,0:T(8,128)(2,1)}, bf16[2,256,3,64]{1,3,2,0:T(8,128)(2,1)}, u32[]{:S(2)}, u32[]{:S(2)}) collective-permute-start(bf16[2,256,3,64]{1,3,2,0:T(8,128)(2,1)} %fusion.109), channel_id=1, source_target_pairs={{0,4},{4,8},{8,12},{12,16},{16,20},{20,24},{24,28},{28,0},{1,5},{5... | collective-permute-start | bytes 589832 | tf_op jit(solution)/shard_map/while/body/eval_jaxpr/ppermute | solution.py:13
  471.9 14.8 %collective-permute-start.3 = (bf16[2,256,3,64]{1,3,2,0:T(8,128)(2,1)}, bf16[2,256,3,64]{1,3,2,0:T(8,128)(2,1)S(1)}, u32[]{:S(2)}, u32[]{:S(2)}) collective-permute-start(bf16[2,256,3,64]{1,3,2,0:T(8,128)(2,1)} %fusion.110), channel_id=1, source_target_pairs={{0,4},{4,8},{8,12},{12,16},{16,20},{20,24},{24,28},{28,0},{1,5},{5... | collective-permute-start | bytes 589832 | tf_op jit(solution)/shard_map/while/body/eval_jaxpr/ppermute | solution.py:13
  488.4 19.0 %collective-permute-start = (bf16[2,256,3,64]{1,3,2,0:T(8,128)(2,1)S(1)}, bf16[2,256,3,64]{1,3,2,0:T(8,128)(2,1)}, u32[]{:S(2)}, u32[]{:S(2)}) collective-permute-start(bf16[2,256,3,64]{1,3,2,0:T(8,128)(2,1)S(1)} %copy.62), channel_id=1, source_target_pairs={{0,4},{4,8},{8,12},{12,16},{16,20},{20,24},{24,28},{28,0},{1,5},{5... | collective-permute-start | bytes 589832 | tf_op jit(solution)/shard_map/while/body/eval_jaxpr/ppermute | solution.py:13
  489.3 18.1 %collective-permute-start.1 = (bf16[2,256,3,64]{1,3,2,0:T(8,128)(2,1)S(1)}, bf16[2,256,3,64]{1,3,2,0:T(8,128)(2,1)}, u32[]{:S(2)}, u32[]{:S(2)}) collective-permute-start(bf16[2,256,3,64]{1,3,2,0:T(8,128)(2,1)S(1)} %copy.63), channel_id=1, source_target_pairs={{0,4},{4,8},{8,12},{12,16},{16,20},{20,24},{24,28},{28,0},{1,5},{5... | collective-permute-start | bytes 589832 | tf_op jit(solution)/shard_map/while/body/eval_jaxpr/ppermute | solution.py:13
  492.4 12.2 %collective-permute-start.2 = (bf16[2,256,3,64]{1,3,2,0:T(8,128)(2,1)}, bf16[2,256,3,64]{1,3,2,0:T(8,128)(2,1)}, u32[]{:S(2)}, u32[]{:S(2)}) collective-permute-start(bf16[2,256,3,64]{1,3,2,0:T(8,128)(2,1)} %fusion.109), channel_id=1, source_target_pairs={{0,4},{4,8},{8,12},{12,16},{16,20},{20,24},{24,28},{28,0},{1,5},{5... | collective-permute-start | bytes 589832 | tf_op jit(solution)/shard_map/while/body/eval_jaxpr/ppermute | solution.py:13
  494.5 12.2 %collective-permute-start.3 = (bf16[2,256,3,64]{1,3,2,0:T(8,128)(2,1)}, bf16[2,256,3,64]{1,3,2,0:T(8,128)(2,1)S(1)}, u32[]{:S(2)}, u32[]{:S(2)}) collective-permute-start(bf16[2,256,3,64]{1,3,2,0:T(8,128)(2,1)} %fusion.110), channel_id=1, source_target_pairs={{0,4},{4,8},{8,12},{12,16},{16,20},{20,24},{24,28},{28,0},{1,5},{5... | collective-permute-start | bytes 589832 | tf_op jit(solution)/shard_map/while/body/eval_jaxpr/ppermute | solution.py:13
  508.4 18.2 %collective-permute-start = (bf16[2,256,3,64]{1,3,2,0:T(8,128)(2,1)S(1)}, bf16[2,256,3,64]{1,3,2,0:T(8,128)(2,1)}, u32[]{:S(2)}, u32[]{:S(2)}) collective-permute-start(bf16[2,256,3,64]{1,3,2,0:T(8,128)(2,1)S(1)} %copy.62), channel_id=1, source_target_pairs={{0,4},{4,8},{8,12},{12,16},{16,20},{20,24},{24,28},{28,0},{1,5},{5... | collective-permute-start | bytes 589832 | tf_op jit(solution)/shard_map/while/body/eval_jaxpr/ppermute | solution.py:13
  509.3 17.3 %collective-permute-start.1 = (bf16[2,256,3,64]{1,3,2,0:T(8,128)(2,1)S(1)}, bf16[2,256,3,64]{1,3,2,0:T(8,128)(2,1)}, u32[]{:S(2)}, u32[]{:S(2)}) collective-permute-start(bf16[2,256,3,64]{1,3,2,0:T(8,128)(2,1)S(1)} %copy.63), channel_id=1, source_target_pairs={{0,4},{4,8},{8,12},{12,16},{16,20},{20,24},{24,28},{28,0},{1,5},{5... | collective-permute-start | bytes 589832 | tf_op jit(solution)/shard_map/while/body/eval_jaxpr/ppermute | solution.py:13
  512.4 11.4 %collective-permute-start.2 = (bf16[2,256,3,64]{1,3,2,0:T(8,128)(2,1)}, bf16[2,256,3,64]{1,3,2,0:T(8,128)(2,1)}, u32[]{:S(2)}, u32[]{:S(2)}) collective-permute-start(bf16[2,256,3,64]{1,3,2,0:T(8,128)(2,1)} %fusion.109), channel_id=1, source_target_pairs={{0,4},{4,8},{8,12},{12,16},{16,20},{20,24},{24,28},{28,0},{1,5},{5... | collective-permute-start | bytes 589832 | tf_op jit(solution)/shard_map/while/body/eval_jaxpr/ppermute | solution.py:13
  514.4 11.3 %collective-permute-start.3 = (bf16[2,256,3,64]{1,3,2,0:T(8,128)(2,1)}, bf16[2,256,3,64]{1,3,2,0:T(8,128)(2,1)S(1)}, u32[]{:S(2)}, u32[]{:S(2)}) collective-permute-start(bf16[2,256,3,64]{1,3,2,0:T(8,128)(2,1)} %fusion.110), channel_id=1, source_target_pairs={{0,4},{4,8},{8,12},{12,16},{16,20},{20,24},{24,28},{28,0},{1,5},{5... | collective-permute-start | bytes 589832 | tf_op jit(solution)/shard_map/while/body/eval_jaxpr/ppermute | solution.py:13
  527.6 18.5 %collective-permute-start = (bf16[2,256,3,64]{1,3,2,0:T(8,128)(2,1)S(1)}, bf16[2,256,3,64]{1,3,2,0:T(8,128)(2,1)}, u32[]{:S(2)}, u32[]{:S(2)}) collective-permute-start(bf16[2,256,3,64]{1,3,2,0:T(8,128)(2,1)S(1)} %copy.62), channel_id=1, source_target_pairs={{0,4},{4,8},{8,12},{12,16},{16,20},{20,24},{24,28},{28,0},{1,5},{5... | collective-permute-start | bytes 589832 | tf_op jit(solution)/shard_map/while/body/eval_jaxpr/ppermute | solution.py:13
  528.5 17.6 %collective-permute-start.1 = (bf16[2,256,3,64]{1,3,2,0:T(8,128)(2,1)S(1)}, bf16[2,256,3,64]{1,3,2,0:T(8,128)(2,1)}, u32[]{:S(2)}, u32[]{:S(2)}) collective-permute-start(bf16[2,256,3,64]{1,3,2,0:T(8,128)(2,1)S(1)} %copy.63), channel_id=1, source_target_pairs={{0,4},{4,8},{8,12},{12,16},{16,20},{20,24},{24,28},{28,0},{1,5},{5... | collective-permute-start | bytes 589832 | tf_op jit(solution)/shard_map/while/body/eval_jaxpr/ppermute | solution.py:13
  534.4 8.7 %collective-permute-start.2 = (bf16[2,256,3,64]{1,3,2,0:T(8,128)(2,1)}, bf16[2,256,3,64]{1,3,2,0:T(8,128)(2,1)}, u32[]{:S(2)}, u32[]{:S(2)}) collective-permute-start(bf16[2,256,3,64]{1,3,2,0:T(8,128)(2,1)} %fusion.109), channel_id=1, source_target_pairs={{0,4},{4,8},{8,12},{12,16},{16,20},{20,24},{24,28},{28,0},{1,5},{5... | collective-permute-start | bytes 589832 | tf_op jit(solution)/shard_map/while/body/eval_jaxpr/ppermute | solution.py:13
  536.4 8.8 %collective-permute-start.3 = (bf16[2,256,3,64]{1,3,2,0:T(8,128)(2,1)}, bf16[2,256,3,64]{1,3,2,0:T(8,128)(2,1)S(1)}, u32[]{:S(2)}, u32[]{:S(2)}) collective-permute-start(bf16[2,256,3,64]{1,3,2,0:T(8,128)(2,1)} %fusion.110), channel_id=1, source_target_pairs={{0,4},{4,8},{8,12},{12,16},{16,20},{20,24},{24,28},{28,0},{1,5},{5... | collective-permute-start | bytes 589832 | tf_op jit(solution)/shard_map/while/body/eval_jaxpr/ppermute | solution.py:13
  547.0 25.2 %collective-permute-start = (bf16[2,256,3,64]{1,3,2,0:T(8,128)(2,1)S(1)}, bf16[2,256,3,64]{1,3,2,0:T(8,128)(2,1)}, u32[]{:S(2)}, u32[]{:S(2)}) collective-permute-start(bf16[2,256,3,64]{1,3,2,0:T(8,128)(2,1)S(1)} %copy.62), channel_id=1, source_target_pairs={{0,4},{4,8},{8,12},{12,16},{16,20},{20,24},{24,28},{28,0},{1,5},{5... | collective-permute-start | bytes 589832 | tf_op jit(solution)/shard_map/while/body/eval_jaxpr/ppermute | solution.py:13
  547.9 24.3 %collective-permute-start.1 = (bf16[2,256,3,64]{1,3,2,0:T(8,128)(2,1)S(1)}, bf16[2,256,3,64]{1,3,2,0:T(8,128)(2,1)}, u32[]{:S(2)}, u32[]{:S(2)}) collective-permute-start(bf16[2,256,3,64]{1,3,2,0:T(8,128)(2,1)S(1)} %copy.63), channel_id=1, source_target_pairs={{0,4},{4,8},{8,12},{12,16},{16,20},{20,24},{24,28},{28,0},{1,5},{5... | collective-permute-start | bytes 589832 | tf_op jit(solution)/shard_map/while/body/eval_jaxpr/ppermute | solution.py:13
  551.8 17.6 %collective-permute-start.2 = (bf16[2,256,3,64]{1,3,2,0:T(8,128)(2,1)}, bf16[2,256,3,64]{1,3,2,0:T(8,128)(2,1)}, u32[]{:S(2)}, u32[]{:S(2)}) collective-permute-start(bf16[2,256,3,64]{1,3,2,0:T(8,128)(2,1)} %fusion.109), channel_id=1, source_target_pairs={{0,4},{4,8},{8,12},{12,16},{16,20},{20,24},{24,28},{28,0},{1,5},{5... | collective-permute-start | bytes 589832 | tf_op jit(solution)/shard_map/while/body/eval_jaxpr/ppermute | solution.py:13
  554.4 17.0 %collective-permute-start.3 = (bf16[2,256,3,64]{1,3,2,0:T(8,128)(2,1)}, bf16[2,256,3,64]{1,3,2,0:T(8,128)(2,1)S(1)}, u32[]{:S(2)}, u32[]{:S(2)}) collective-permute-start(bf16[2,256,3,64]{1,3,2,0:T(8,128)(2,1)} %fusion.110), channel_id=1, source_target_pairs={{0,4},{4,8},{8,12},{12,16},{16,20},{20,24},{24,28},{28,0},{1,5},{5... | collective-permute-start | bytes 589832 | tf_op jit(solution)/shard_map/while/body/eval_jaxpr/ppermute | solution.py:13
  575.7 7.2 copy-start.22
  575.7 7.2 copy-start.31
  575.7 7.2 copy-start.37
  577.6 16.9 %all-to-all-start.3 = ((bf16[2,256,3,1,192]{4,0,3,2,1:T(2,128)(2,1)}), bf16[2,256,3,1,192]{4,0,3,2,1:T(2,128)(2,1)S(1)}, u32[]{:S(2)}, u32[]{:S(2)}) async-start(bf16[2,256,3,1,192]{4,0,3,2,1:T(2,128)(2,1)} %copy.48), calls=%async_computation.3 | async-start | bytes 1572864 | tf_op jit(solution)/shard_map/all_to_all | solution.py:207
  582.9 278.1 %reduce-scatter.7.cloned.1.call-start = ((), (), s32[]{:S(2)}) async-start(), calls=%async_computation.13 | async-start | bytes 7299072 | tf_op jit(solution)/shard_map/reduce_scatter | solution.py:217
  602.9 41.6 %copy-start.7 = (f32[128,768]{1,0:T(8,128)S(1)}, f32[128,768]{1,0:T(8,128)}, u32[]{:S(2)}) copy-start(f32[128,768]{1,0:T(8,128)} %copy-done.6) | copy-start | bytes 1179652
  (48 other events, 122.1 us)
Sparse Core Ops, SparseCore 0:
  10.9 62.8 all-gather.7
  96.7 44.0 all-gather.9
  143.4 43.4 all-gather.17
  189.7 52.2 all-gather.11
  244.8 59.0 all-gather.13
  306.6 54.4 all-gather.15
  368.8 114.1 reduce-scatter.8
  489.9 121.3 reduce-scatter.12
  618.6 117.8 reduce-scatter.10
  742.6 118.4 reduce-scatter.6
where the time goes:
time: 870 us; the launch traced here: 868 us
  waiting for transfers between devices  570 us (66%)
  matrix products  99.2 us (11%)
  blocking collectives  79.2 us (9%)
  local copies, waits for them, and re-layouts  36 us (4%)
  other arithmetic  35.4 us (4%)
  starting transfers between devices  32.5 us (4%)
  between operations  14.8 us (2%)
    reduce_scatter x1, waiting for transfers between devices, body(): lax.psum_scatter(grad_wqkv, ('blk', 'ulysses'), scatter_dimension=0, tile...  125 us
    reduce_scatter x1, waiting for transfers between devices, body(): lax.psum_scatter(grad_win, ('blk', 'ulysses'), scatter_dimension=0, tiled...  91 us
    unnamed x2, blocking collectives  79.2 us
    ppermute x32, waiting for transfers between devices, from_behind(): lax.ppermute(value, axis, [(i, (i + by) % size) for i in range(size)])  76.3 us
    all_gather x1, waiting for transfers between devices, body(): lax.all_gather(in_weight, ('blk', 'ulysses'), axis=0, tiled=True)  59.9 us
    all_gather x1, waiting for transfers between devices, body(): lax.all_gather(out_weight, ('blk', 'ulysses'), axis=1, tiled=True)  54.5 us
    all_gather x1, waiting for transfers between devices, body(): key_piece = lax.all_gather(key_rows, 'blk', axis=1, tiled=True)  41.7 us
    all_gather x1, waiting for transfers between devices, body(): lax.all_gather(attn_out_weight, ('blk', 'ulysses'), axis=0, tiled=True)  36.1 us
  transfers between devices with their start and end apart: 46, of which 28 were waited for; matrix products, arithmetic and copies ran while one was open for 17% of the time, Pallas kernels for 0%

commit v1 on v0

--- a/solution.py
+++ b/solution.py
@@ -105,7 +105,12 @@
     value_rows = headwise[:, :, 2]
     start_top = jnp.full((sequences, heads_here, group_rows), -1e30, jnp.float32)
     zeros_rows = jnp.zeros((sequences, group_rows, heads_here, HEAD), jnp.float32)
-    key_piece = lax.all_gather(key_rows, "blk", axis=1, tiled=True)
+    ring = [key_rows]
+    for hop in range(7):
+        ring.append(lax.ppermute(ring[-1], "blk", [(dev, (dev + 1) % 8) for dev in range(8)]))
+    key_piece = jnp.roll(
+        jnp.concatenate(ring[::-1], axis=1), (lax.axis_index("blk") + 1) * ring[0].shape[1], axis=1
+    )
     value_piece = lax.all_gather(value_rows, "blk", axis=1, tiled=True)
     scores = (
         jnp.einsum("sqhd,skhd->shqk", queries, key_piece, preferred_element_type=jnp.float32)

time: 870 us -> 828 us (0.952)
  waiting for transfers between devices: 570 us -> 510 us
  blocking collectives: 79.2 us -> 93.3 us
  matrix products: 99.2 us -> 109 us
  local copies, waits for them, and re-layouts: 36 us -> 27 us
    ppermute x0 -> x7, waiting for transfers between devices: none -> 66 us  [body(): lax.ppermute(ring[-1], 'blk', [(dev, (dev + 1) % 8) for dev in range(8)])]
    all_gather x1 -> x0, waiting for transfers between devices: 41.7 us -> none  [body(): key_piece = lax.all_gather(key_rows, 'blk', axis=1, tiled=True)]
    all_gather x1, waiting for transfers between devices: 35.8 us -> 0.02 us  [body(): value_piece = lax.all_gather(value_rows, 'blk', axis=1, tiled=True)]
    all_gather x1, waiting for transfers between devices: 36.1 us -> 7.02 us  [body(): lax.all_gather(attn_out_weight, ('blk', 'ulysses'), axis=0, tiled=True)]
    all_to_all x0 -> x1, blocking collectives: none -> 14.2 us  [body(): lax.all_to_all(packed, 'ulysses', split_axis=3, concat_axis=1, tiled=True)]
    all_to_all x1 -> x0, waiting for transfers between devices: 10.7 us -> none  [body(): lax.all_to_all(packed, 'ulysses', split_axis=3, concat_axis=1, tiled=True)]
  transfers between devices with their start and end apart: 46 -> 51, of which waited for: 28 -> 32; matrix products, arithmetic and copies ran while one was open for 17% -> 18% of each run, Pallas kernels for 0% -> 0%
where the time goes in v1:
time: 828 us; the launch traced here: 826 us
  waiting for transfers between devices  510 us (62%)
  matrix products  109 us (13%)
  blocking collectives  93.3 us (11%)
  starting transfers between devices  36.6 us (4%)
  other arithmetic  36.2 us (4%)
  local copies, waits for them, and re-layouts  27 us (3%)
  between operations  14.6 us (2%)
    reduce_scatter x1, waiting for transfers between devices, body(): lax.psum_scatter(grad_wqkv, ('blk', 'ulysses'), scatter_dimension=0, tile...  125 us
    reduce_scatter x1, waiting for transfers between devices, body(): lax.psum_scatter(grad_win, ('blk', 'ulysses'), scatter_dimension=0, tiled...  87.9 us
    unnamed x2, blocking collectives  79.1 us
    ppermute x32, waiting for transfers between devices, from_behind(): lax.ppermute(value, axis, [(i, (i + by) % size) for i in range(size)])  69.1 us
    ppermute x7, waiting for transfers between devices, body(): lax.ppermute(ring[-1], 'blk', [(dev, (dev + 1) % 8) for dev in range(8)])  66 us
    all_gather x1, waiting for transfers between devices, body(): lax.all_gather(in_weight, ('blk', 'ulysses'), axis=0, tiled=True)  59.9 us
    all_gather x1, waiting for transfers between devices, body(): lax.all_gather(out_weight, ('blk', 'ulysses'), axis=1, tiled=True)  54.5 us
    ppermute x32, starting transfers between devices, from_behind(): lax.ppermute(value, axis, [(i, (i + by) % size) for i in range(size)])  21.3 us
  transfers between devices with their start and end apart: 51, of which 32 were waited for; matrix products, arithmetic and copies ran while one was open for 18% of the time, Pallas kernels for 0%

profile of v1, /device:TPU:0, one launch (start us, length us, event | category | flops | bytes accessed | tf_op | source)
XLA Modules:
  0.0 826.0 jit_solution(14625606097439817447)
XLA Ops:
  9.6 42.1 %all-reduce.8 = (bf16[768]{0:T(1024)(128)(2,1)S(1)}, bf16[768]{0:T(1024)(128)(2,1)S(1)}) all-reduce(bf16[768]{0:T(1024)(128)(2,1)S(1)} %dynamic-update-slice, bf16[768]{0:T(1024)(128)(2,1)S(1)} %dynamic-update-slice.1), channel_id=1, replica_groups=mesh['blk'=8,'ulysses'=4] {'blk','ulysses'}, use_global_device_ids=true, to_apply=%add.2 | all-reduce | flops 1536 | bytes 6144
  55.8 18.0 %all-gather.7.cloned.1.call-done = bf16[768,2304]{1,0:T(8,128)(2,1)} async-done(((bf16[24,2304]{1,0:T(8,128)(2,1)}), bf16[768,2304]{1,0:T(8,128)(2,1)}) %all-gather.7.cloned.1.call-update) | async-done | bytes 3538960 | tf_op jit(solution)/shard_map/all_gather | solution.py:81
  73.8 2.6 convolution_convert_fusion
  77.4 14.2 %all_to_all.60 = bf16[2,64,3,4,192]{4,1,2,0,3:T(8,128)(2,1)S(1)} all-to-all(bf16[2,64,3,4,192]{4,1,2,0,3:T(8,128)(2,1)S(1)} %copy.38), channel_id=1, replica_groups=mesh['blk'=8,'ulysses'=4] {'ulysses'}, dimensions={3} | all-to-all | bytes 1179648 | tf_op jit(solution)/shard_map/all_to_all | solution.py:96
  97.7 7.8 collective-permute-done.4
  105.5 10.1 %collective-permute-done.5 = bf16[2,256,3,64]{1,3,2,0:T(8,128)(2,1)S(1)} collective-permute-done((bf16[2,256,3,64]{1,3,2,0:T(8,128)(2,1)S(1)}, bf16[2,256,3,64]{1,3,2,0:T(8,128)(2,1)S(1)}, u32[]{:S(2)}, u32[]{:S(2)}) %collective-permute-start.5) | collective-permute-done | bytes 196640 | tf_op jit(solution)/shard_map/ppermute | solution.py:110
  115.7 8.4 %collective-permute-done.6 = bf16[2,256,3,64]{1,3,2,0:T(8,128)(2,1)S(1)} collective-permute-done((bf16[2,256,3,64]{1,3,2,0:T(8,128)(2,1)S(1)}, bf16[2,256,3,64]{1,3,2,0:T(8,128)(2,1)S(1)}, u32[]{:S(2)}, u32[]{:S(2)}) %collective-permute-start.6) | collective-permute-done | bytes 196640 | tf_op jit(solution)/shard_map/ppermute | solution.py:110
  124.1 11.0 %collective-permute-done.7 = bf16[2,256,3,64]{1,3,2,0:T(8,128)(2,1)S(1)} collective-permute-done((bf16[2,256,3,64]{1,3,2,0:T(8,128)(2,1)S(1)}, bf16[2,256,3,64]{1,3,2,0:T(8,128)(2,1)S(1)}, u32[]{:S(2)}, u32[]{:S(2)}) %collective-permute-start.7) | collective-permute-done | bytes 196640 | tf_op jit(solution)/shard_map/ppermute | solution.py:110
  135.2 11.5 %collective-permute-done.8 = bf16[2,256,3,64]{1,3,2,0:T(8,128)(2,1)S(1)} collective-permute-done((bf16[2,256,3,64]{1,3,2,0:T(8,128)(2,1)S(1)}, bf16[2,256,3,64]{1,3,2,0:T(8,128)(2,1)S(1)}, u32[]{:S(2)}, u32[]{:S(2)}) %collective-permute-start.8) | collective-permute-done | bytes 196640 | tf_op jit(solution)/shard_map/ppermute | solution.py:110
  146.8 8.6 %collective-permute-done.9 = bf16[2,256,3,64]{1,3,2,0:T(8,128)(2,1)S(1)} collective-permute-done((bf16[2,256,3,64]{1,3,2,0:T(8,128)(2,1)S(1)}, bf16[2,256,3,64]{1,3,2,0:T(8,128)(2,1)S(1)}, u32[]{:S(2)}, u32[]{:S(2)}) %collective-permute-start.9) | collective-permute-done | bytes 196640 | tf_op jit(solution)/shard_map/ppermute | solution.py:110
  155.4 8.5 %collective-permute-done.10 = bf16[2,256,3,64]{1,3,2,0:T(8,128)(2,1)S(1)} collective-permute-done((bf16[2,256,3,64]{1,3,2,0:T(8,128)(2,1)S(1)}, bf16[2,256,3,64]{1,3,2,0:T(8,128)(2,1)S(1)}, u32[]{:S(2)}, u32[]{:S(2)}) %collective-permute-start.10) | collective-permute-done | bytes 196640 | tf_op jit(solution)/shard_map/ppermute | solution.py:110
  166.3 4.5 copy-done
  170.8 2.4 fusion.11
  173.3 8.2 fusion.59
  182.4 6.3 all-to-all-start.1
  188.7 8.1 all-to-all-done.1
  197.3 7.0 all-gather.9.cloned.1.call-done
  206.3 59.9 %all-gather.11.cloned.1.call-done = bf16[768,2304]{1,0:T(8,128)(2,1)} async-done(((bf16[24,2304]{1,0:T(8,128)(2,1)}), bf16[768,2304]{1,0:T(8,128)(2,1)}) %all-gather.11.cloned.1.call-update) | async-done | bytes 3538960 | tf_op jit(solution)/shard_map/all_gather | solution.py:83
  266.1 2.7 fusion.57
  268.8 54.5 %all-gather.13.cloned.1.call-done = bf16[1152,768]{0,1:T(8,128)(2,1)} async-done(((bf16[1152,24]{0,1:T(8,128)(2,1)}), bf16[1152,768]{0,1:T(8,128)(2,1)}) %all-gather.13.cloned.1.call-update) | async-done | bytes 1769488 | tf_op jit(solution)/shard_map/all_gather | solution.py:84
  323.3 3.2 fusion.47
  331.0 3.5 fusion.62
  338.5 3.4 all-to-all-start.2
  342.0 4.7 fusion.51
  350.1 183.2 %while.19 = (s32[]{:T(128)}, bf16[2,256,3,64]{1,3,2,0:T(8,128)(2,1)S(1)}, bf16[2,256,3,64]{1,3,2,0:T(8,128)(2,1)}, f32[2,256,3,64]{1,3,2,0:T(8,128)}, f32[2,256,...) while((s32[]{:T(128)}, ...), condition=%wide.region_10.11_spmd.clone, body=%wide.region_9.10_spmd.clone.sunk | while | flops 255787008 | bytes 15556913 | solution.py:204
  357.4 2.1 fusion.112
  361.6 7.7 collective-permute-done.2
  376.0 1.9 fusion.111
  378.4 2.2 fusion.112
  382.5 2.2 fusion.113
  384.6 12.8 %collective-permute-done.2 = bf16[2,256,3,64]{1,3,2,0:T(8,128)(2,1)} collective-permute-done((bf16[2,256,3,64]{1,3,2,0:T(8,128)(2,1)}, bf16[2,256,3,64]{1,3,2,0:T(8,128)(2,1)}, u32[]{:S(2)}, u32[]{:S(2)}) %collective-permute-start.2) | collective-permute-done | bytes 196640 | tf_op jit(solution)/shard_map/while/body/eval_jaxpr/ppermute | solution.py:13
  405.9 2.3 fusion.112
  408.2 2.2 fusion.113
  410.4 10.7 %collective-permute-done.2 = bf16[2,256,3,64]{1,3,2,0:T(8,128)(2,1)} collective-permute-done((bf16[2,256,3,64]{1,3,2,0:T(8,128)(2,1)}, bf16[2,256,3,64]{1,3,2,0:T(8,128)(2,1)}, u32[]{:S(2)}, u32[]{:S(2)}) %collective-permute-start.2) | collective-permute-done | bytes 196640 | tf_op jit(solution)/shard_map/while/body/eval_jaxpr/ppermute | solution.py:13
  429.0 2.2 fusion.112
  431.3 2.2 fusion.113
  433.4 9.1 %collective-permute-done.2 = bf16[2,256,3,64]{1,3,2,0:T(8,128)(2,1)} collective-permute-done((bf16[2,256,3,64]{1,3,2,0:T(8,128)(2,1)}, bf16[2,256,3,64]{1,3,2,0:T(8,128)(2,1)}, u32[]{:S(2)}, u32[]{:S(2)}) %collective-permute-start.2) | collective-permute-done | bytes 196640 | tf_op jit(solution)/shard_map/while/body/eval_jaxpr/ppermute | solution.py:13
  450.5 2.2 fusion.112
  452.7 2.4 collective-permute-start.3
  455.1 2.2 fusion.113
  457.3 5.2 collective-permute-done.2
  469.6 2.0 fusion.111
  471.6 2.2 fusion.112
  473.8 2.8 collective-permute-start.3
  476.7 2.2 fusion.113
  478.8 3.4 collective-permute-done.2
  486.1 3.2 collective-permute-start.1
  491.3 2.0 fusion.111
  493.3 2.2 fusion.112
  495.5 2.2 fusion.113
  497.7 4.4 collective-permute-done.2
  509.0 2.0 fusion.111
  510.9 2.2 fusion.112
  513.2 3.4 collective-permute-start.3
  516.6 2.2 fusion.113
  518.7 11.3 %collective-permute-done.2 = bf16[2,256,3,64]{1,3,2,0:T(8,128)(2,1)} collective-permute-done((bf16[2,256,3,64]{1,3,2,0:T(8,128)(2,1)}, bf16[2,256,3,64]{1,3,2,0:T(8,128)(2,1)}, u32[]{:S(2)}, u32[]{:S(2)}) %collective-permute-start.2) | collective-permute-done | bytes 196640 | tf_op jit(solution)/shard_map/while/body/eval_jaxpr/ppermute | solution.py:13
  540.0 3.6 all-to-all-start.3
  544.0 11.3 %all-to-all-done.3 = bf16[2,256,3,1,192]{4,0,3,2,1:T(2,128)(2,1)S(1)} async-done(((bf16[2,256,3,1,192]{4,0,3,2,1:T(2,128)(2,1)}), bf16[2,256,3,1,192]{4,0,3,2,1:T(2,128)(2,1)S(1)}, u32[]{:S(2)}, u32[]{:S(2)}) %all-to-all-start.3) | async-done | bytes 589856 | tf_op jit(solution)/shard_map/all_to_all | solution.py:212
  556.7 4.0 fusion.61
  561.7 2.9 fusion.23
  564.5 3.4 multiply_reduce_fusion.2
  568.0 37.0 %all-reduce.7 = (f32[768]{0:T(1024)S(1)}, f32[768]{0:T(1024)S(1)}) all-reduce(f32[768]{0:T(1024)S(1)} %get-tuple-element.116, f32[768]{0:T(1024)S(1)} %copy-done.20), channel_id=3, replica_groups=mesh['blk'=8,'ulysses'=4] {'blk','ulysses'}, use_global_device_ids=true, to_apply=%region_14.15.clone | all-reduce | flops 1536 | bytes 12288
  607.0 87.9 %reduce-scatter.11.cloned.1.call-done = f32[24,2304]{1,0:T(8,128)} async-done(((f32[768,2304]{1,0:T(8,128)}), f32[24,2304]{1,0:T(8,128)}) %reduce-scatter.11.cloned.1.call-update) | async-done | bytes 221200 | tf_op jit(solution)/shard_map/reduce_scatter | solution.py:224
  694.9 124.6 %reduce-scatter.7.cloned.1.call-done = f32[24,2304]{1,0:T(8,128)} async-done(((f32[768,2304]{1,0:T(8,128)}), f32[24,2304]{1,0:T(8,128)}) %reduce-scatter.7.cloned.1.call-update) | async-done | bytes 221200 | tf_op jit(solution)/shard_map/reduce_scatter | solution.py:222
  (275 shorter events, 108.1 us)
Async XLA Ops:
  7.2 66.7 %all-gather.7.cloned.1.call-start = ((), (), s32[]{:S(2)}) async-start(), calls=%async_computation.8 | async-start | bytes 3649536 | tf_op jit(solution)/shard_map/all_gather | solution.py:81
  7.9 165.4 %all-gather.15.cloned.1.call-start = ((), (), s32[]{:S(2)}) async-start(), calls=%async_computation.15 | async-start | bytes 1769472 | tf_op jit(solution)/shard_map/all_gather | solution.py:114
  51.8 22.0 %copy-start.15 = (f32[768]{0:T(1024)}, f32[768]{0:T(1024)S(1)}, u32[]{:S(2)}) copy-start(f32[768]{0:T(1024)S(1)} %convert_element_type.109) | copy-start | bytes 9220
  52.9 20.9 %copy-start.24 = (f32[128]{0:T(128)}, f32[128]{0:T(128)S(1)}, u32[]{:S(2)}) copy-start(f32[128]{0:T(128)S(1)} %div.49) | copy-start | bytes 1540
  54.7 19.1 %copy-start.26 = (f32[128]{0:T(128)}, f32[128]{0:T(128)S(1)}, u32[]{:S(2)}) copy-start(f32[128]{0:T(128)S(1)} %rsqrt.21) | copy-start | bytes 1540
  93.9 110.5 %all-gather.9.cloned.1.call-start = ((), (), s32[]{:S(2)}) async-start(), calls=%async_computation.9 | async-start | bytes 1216512 | tf_op jit(solution)/shard_map/all_gather | solution.py:82
  94.6 171.5 %all-gather.11.cloned.1.call-start = ((), (), s32[]{:S(2)}) async-start(), calls=%async_computation.10 | async-start | bytes 3649536 | tf_op jit(solution)/shard_map/all_gather | solution.py:83
  95.2 228.1 %all-gather.13.cloned.1.call-start = ((), (), s32[]{:S(2)}) async-start(), calls=%async_computation.11 | async-start | bytes 1824768 | tf_op jit(solution)/shard_map/all_gather | solution.py:84
  95.5 68.6 %copy-start.14 = (f32[256,64]{0,1:T(8,128)}, f32[256,64]{0,1:T(8,128)S(1)}, u32[]{:S(2)}) copy-start(f32[256,64]{0,1:T(8,128)S(1)} %pad_maximum_fusion.1) | copy-start | bytes 196612
  96.4 9.2 %collective-permute-start.4 = (bf16[2,256,3,64]{1,3,2,0:T(8,128)(2,1)S(1)}, bf16[2,256,3,64]{1,3,2,0:T(8,128)(2,1)S(1)}, u32[]{:S(2)}, u32[]{:S(2)}) collective-permute-start(bf16[2,256,3,64]{1,3,2,0:T(8,128)(2,1)S(1)} %get-tuple-element.257), channel_id=1, source_target_pairs={{0,4},{4,8},{8,12},{12,16},{16,20},{20,24},{24,28},{28,0},{1,5},{5... | collective-permute-start | bytes 589832 | tf_op jit(solution)/shard_map/ppermute | solution.py:110
  105.5 10.1 %collective-permute-start.5 = (bf16[2,256,3,64]{1,3,2,0:T(8,128)(2,1)S(1)}, bf16[2,256,3,64]{1,3,2,0:T(8,128)(2,1)S(1)}, u32[]{:S(2)}, u32[]{:S(2)}) collective-permute-start(bf16[2,256,3,64]{1,3,2,0:T(8,128)(2,1)S(1)} %collective-permute-done.4), channel_id=1, source_target_pairs={{0,4},{4,8},{8,12},{12,16},{16,20},{20,24},{24,28},{28,0},{1,5},{5... | collective-permute-start | bytes 589832 | tf_op jit(solution)/shard_map/ppermute | solution.py:110
  115.7 8.4 %collective-permute-start.6 = (bf16[2,256,3,64]{1,3,2,0:T(8,128)(2,1)S(1)}, bf16[2,256,3,64]{1,3,2,0:T(8,128)(2,1)S(1)}, u32[]{:S(2)}, u32[]{:S(2)}) collective-permute-start(bf16[2,256,3,64]{1,3,2,0:T(8,128)(2,1)S(1)} %collective-permute-done.5), channel_id=1, source_target_pairs={{0,4},{4,8},{8,12},{12,16},{16,20},{20,24},{24,28},{28,0},{1,5},{5... | collective-permute-start | bytes 589832 | tf_op jit(solution)/shard_map/ppermute | solution.py:110
  124.0 11.0 %collective-permute-start.7 = (bf16[2,256,3,64]{1,3,2,0:T(8,128)(2,1)S(1)}, bf16[2,256,3,64]{1,3,2,0:T(8,128)(2,1)S(1)}, u32[]{:S(2)}, u32[]{:S(2)}) collective-permute-start(bf16[2,256,3,64]{1,3,2,0:T(8,128)(2,1)S(1)} %collective-permute-done.6), channel_id=1, source_target_pairs={{0,4},{4,8},{8,12},{12,16},{16,20},{20,24},{24,28},{28,0},{1,5},{5... | collective-permute-start | bytes 589832 | tf_op jit(solution)/shard_map/ppermute | solution.py:110
  135.0 11.8 %collective-permute-start.8 = (bf16[2,256,3,64]{1,3,2,0:T(8,128)(2,1)S(1)}, bf16[2,256,3,64]{1,3,2,0:T(8,128)(2,1)S(1)}, u32[]{:S(2)}, u32[]{:S(2)}) collective-permute-start(bf16[2,256,3,64]{1,3,2,0:T(8,128)(2,1)S(1)} %collective-permute-done.7), channel_id=1, source_target_pairs={{0,4},{4,8},{8,12},{12,16},{16,20},{20,24},{24,28},{28,0},{1,5},{5... | collective-permute-start | bytes 589832 | tf_op jit(solution)/shard_map/ppermute | solution.py:110
  146.8 8.6 %collective-permute-start.9 = (bf16[2,256,3,64]{1,3,2,0:T(8,128)(2,1)S(1)}, bf16[2,256,3,64]{1,3,2,0:T(8,128)(2,1)S(1)}, u32[]{:S(2)}, u32[]{:S(2)}) collective-permute-start(bf16[2,256,3,64]{1,3,2,0:T(8,128)(2,1)S(1)} %collective-permute-done.8), channel_id=1, source_target_pairs={{0,4},{4,8},{8,12},{12,16},{16,20},{20,24},{24,28},{28,0},{1,5},{5... | collective-permute-start | bytes 589832 | tf_op jit(solution)/shard_map/ppermute | solution.py:110
  155.4 8.6 %collective-permute-start.10 = (bf16[2,256,3,64]{1,3,2,0:T(8,128)(2,1)S(1)}, bf16[2,256,3,64]{1,3,2,0:T(8,128)(2,1)S(1)}, u32[]{:S(2)}, u32[]{:S(2)}) collective-permute-start(bf16[2,256,3,64]{1,3,2,0:T(8,128)(2,1)S(1)} %collective-permute-done.9), channel_id=1, source_target_pairs={{0,4},{4,8},{8,12},{12,16},{16,20},{20,24},{24,28},{28,0},{1,5},{5... | collective-permute-start | bytes 589832 | tf_op jit(solution)/shard_map/ppermute | solution.py:110
  173.3 8.3 %copy-start.17 = (f32[2,3,256]{2,1,0:T(4,128)}, f32[2,3,256]{2,1,0:T(4,128)S(1)}, u32[]{:S(2)}) copy-start(f32[2,3,256]{2,1,0:T(4,128)S(1)} %fusion.11) | copy-start | bytes 18436
  173.3 31.0 %copy-start.2 = (bf16[2,64,768]{2,1,0:T(8,128)(2,1)S(1)}, bf16[2,64,768]{2,1,0:T(8,128)(2,1)}, u32[]{:S(2)}) copy-start(bf16[2,64,768]{2,1,0:T(8,128)(2,1)} %param.10) | copy-start | bytes 589828
  182.4 14.4 %all-to-all-start.1 = ((bf16[2,256,1,192]{3,0,2,1:T(2,128)(2,1)}), bf16[2,256,1,192]{3,0,2,1:T(2,128)(2,1)S(1)}, u32[]{:S(2)}, u32[]{:S(2)}) async-start(bf16[2,256,1,192]{3,0,2,1:T(2,128)(2,1)} %copy.43), calls=%async_computation.1 | async-start | bytes 524288 | tf_op jit(solution)/shard_map/all_to_all | solution.py:133
  188.7 418.3 %reduce-scatter.9.cloned.1.call-start = ((), (), s32[]{:S(2)}) async-start(), calls=%async_computation.13 | async-start | bytes 2433024 | tf_op jit(solution)/shard_map/reduce_scatter | solution.py:223
  206.0 117.3 %copy-start.12 = (bf16[2,64,768]{2,1,0:T(8,128)(2,1)S(1)}, bf16[2,64,768]{2,1,0:T(8,128)(2,1)}, u32[]{:S(2)}) copy-start(bf16[2,64,768]{2,1,0:T(8,128)(2,1)} %param.17) | copy-start | bytes 589828
  206.3 122.5 %copy-start.21 = (f32[128]{0:T(128)}, f32[128]{0:T(128)S(1)}, u32[]{:S(2)}) copy-start(f32[128]{0:T(128)S(1)} %add_rsqrt_fusion.1) | copy-start | bytes 1540
  331.0 276.0 %reduce-scatter.13.cloned.1.call-start = ((), (), s32[]{:S(2)}) async-start(), calls=%async_computation.16 | async-start | bytes 3649536
  334.5 7.5 copy-start.10
  338.5 9.4 %all-to-all-start.2 = ((bf16[2,64,4,192]{3,1,0,2:T(8,128)(2,1)}), bf16[2,64,4,192]{3,1,0,2:T(8,128)(2,1)S(1)}, u32[]{:S(2)}, u32[]{:S(2)}) async-start(bf16[2,64,4,192]{3,1,0,2:T(8,128)(2,1)} %copy.46), calls=%async_computation.2 | async-start | bytes 524288 | tf_op jit(solution)/shard_map/all_to_all | solution.py:167
  341.9 352.9 %reduce-scatter.11.cloned.1.call-start = ((), (), s32[]{:S(2)}) async-start(), calls=%async_computation.14 | async-start | bytes 7299072 | tf_op jit(solution)/shard_map/reduce_scatter | solution.py:224
  350.2 22.7 %collective-permute-start = (bf16[2,256,3,64]{1,3,2,0:T(8,128)(2,1)S(1)}, bf16[2,256,3,64]{1,3,2,0:T(8,128)(2,1)S(1)}, u32[]{:S(2)}, u32[]{:S(2)}) collective-permute-start(bf16[2,256,3,64]{1,3,2,0:T(8,128)(2,1)S(1)} %copy.77), channel_id=1, source_target_pairs={{0,4},{4,8},{8,12},{12,16},{16,20},{20,24},{24,28},{28,0},{1,5},{5... | collective-permute-start | bytes 589832 | tf_op jit(solution)/shard_map/while/body/eval_jaxpr/ppermute | solution.py:13
  352.5 20.3 %collective-permute-start.1 = (bf16[2,256,3,64]{1,3,2,0:T(8,128)(2,1)S(1)}, bf16[2,256,3,64]{1,3,2,0:T(8,128)(2,1)}, u32[]{:S(2)}, u32[]{:S(2)}) collective-permute-start(bf16[2,256,3,64]{1,3,2,0:T(8,128)(2,1)S(1)} %copy.78), channel_id=1, source_target_pairs={{0,4},{4,8},{8,12},{12,16},{16,20},{20,24},{24,28},{28,0},{1,5},{5... | collective-permute-start | bytes 589832 | tf_op jit(solution)/shard_map/while/body/eval_jaxpr/ppermute | solution.py:13
  356.1 13.2 %collective-permute-start.2 = (bf16[2,256,3,64]{1,3,2,0:T(8,128)(2,1)}, bf16[2,256,3,64]{1,3,2,0:T(8,128)(2,1)}, u32[]{:S(2)}, u32[]{:S(2)}) collective-permute-start(bf16[2,256,3,64]{1,3,2,0:T(8,128)(2,1)} %fusion.111), channel_id=1, source_target_pairs={{0,4},{4,8},{8,12},{12,16},{16,20},{20,24},{24,28},{28,0},{1,5},{5... | collective-permute-start | bytes 589832 | tf_op jit(solution)/shard_map/while/body/eval_jaxpr/ppermute | solution.py:13
  359.5 12.6 %collective-permute-start.3 = (bf16[2,256,3,64]{1,3,2,0:T(8,128)(2,1)}, bf16[2,256,3,64]{1,3,2,0:T(8,128)(2,1)S(1)}, u32[]{:S(2)}, u32[]{:S(2)}) collective-permute-start(bf16[2,256,3,64]{1,3,2,0:T(8,128)(2,1)} %fusion.112), channel_id=1, source_target_pairs={{0,4},{4,8},{8,12},{12,16},{16,20},{20,24},{24,28},{28,0},{1,5},{5... | collective-permute-start | bytes 589832 | tf_op jit(solution)/shard_map/while/body/eval_jaxpr/ppermute | solution.py:13
  372.9 28.1 %collective-permute-start = (bf16[2,256,3,64]{1,3,2,0:T(8,128)(2,1)S(1)}, bf16[2,256,3,64]{1,3,2,0:T(8,128)(2,1)S(1)}, u32[]{:S(2)}, u32[]{:S(2)}) collective-permute-start(bf16[2,256,3,64]{1,3,2,0:T(8,128)(2,1)S(1)} %copy.77), channel_id=1, source_target_pairs={{0,4},{4,8},{8,12},{12,16},{16,20},{20,24},{24,28},{28,0},{1,5},{5... | collective-permute-start | bytes 589832 | tf_op jit(solution)/shard_map/while/body/eval_jaxpr/ppermute | solution.py:13
  373.9 27.1 %collective-permute-start.1 = (bf16[2,256,3,64]{1,3,2,0:T(8,128)(2,1)S(1)}, bf16[2,256,3,64]{1,3,2,0:T(8,128)(2,1)}, u32[]{:S(2)}, u32[]{:S(2)}) collective-permute-start(bf16[2,256,3,64]{1,3,2,0:T(8,128)(2,1)S(1)} %copy.78), channel_id=1, source_target_pairs={{0,4},{4,8},{8,12},{12,16},{16,20},{20,24},{24,28},{28,0},{1,5},{5... | collective-permute-start | bytes 589832 | tf_op jit(solution)/shard_map/while/body/eval_jaxpr/ppermute | solution.py:13
  377.9 19.5 %collective-permute-start.2 = (bf16[2,256,3,64]{1,3,2,0:T(8,128)(2,1)}, bf16[2,256,3,64]{1,3,2,0:T(8,128)(2,1)}, u32[]{:S(2)}, u32[]{:S(2)}) collective-permute-start(bf16[2,256,3,64]{1,3,2,0:T(8,128)(2,1)} %fusion.111), channel_id=1, source_target_pairs={{0,4},{4,8},{8,12},{12,16},{16,20},{20,24},{24,28},{28,0},{1,5},{5... | collective-permute-start | bytes 589832 | tf_op jit(solution)/shard_map/while/body/eval_jaxpr/ppermute | solution.py:13
  380.6 19.5 %collective-permute-start.3 = (bf16[2,256,3,64]{1,3,2,0:T(8,128)(2,1)}, bf16[2,256,3,64]{1,3,2,0:T(8,128)(2,1)S(1)}, u32[]{:S(2)}, u32[]{:S(2)}) collective-permute-start(bf16[2,256,3,64]{1,3,2,0:T(8,128)(2,1)} %fusion.112), channel_id=1, source_target_pairs={{0,4},{4,8},{8,12},{12,16},{16,20},{20,24},{24,28},{28,0},{1,5},{5... | collective-permute-start | bytes 589832 | tf_op jit(solution)/shard_map/while/body/eval_jaxpr/ppermute | solution.py:13
  401.0 23.1 %collective-permute-start = (bf16[2,256,3,64]{1,3,2,0:T(8,128)(2,1)S(1)}, bf16[2,256,3,64]{1,3,2,0:T(8,128)(2,1)S(1)}, u32[]{:S(2)}, u32[]{:S(2)}) collective-permute-start(bf16[2,256,3,64]{1,3,2,0:T(8,128)(2,1)S(1)} %copy.77), channel_id=1, source_target_pairs={{0,4},{4,8},{8,12},{12,16},{16,20},{20,24},{24,28},{28,0},{1,5},{5... | collective-permute-start | bytes 589832 | tf_op jit(solution)/shard_map/while/body/eval_jaxpr/ppermute | solution.py:13
  402.0 22.1 %collective-permute-start.1 = (bf16[2,256,3,64]{1,3,2,0:T(8,128)(2,1)S(1)}, bf16[2,256,3,64]{1,3,2,0:T(8,128)(2,1)}, u32[]{:S(2)}, u32[]{:S(2)}) collective-permute-start(bf16[2,256,3,64]{1,3,2,0:T(8,128)(2,1)S(1)} %copy.78), channel_id=1, source_target_pairs={{0,4},{4,8},{8,12},{12,16},{16,20},{20,24},{24,28},{28,0},{1,5},{5... | collective-permute-start | bytes 589832 | tf_op jit(solution)/shard_map/while/body/eval_jaxpr/ppermute | solution.py:13
  405.9 15.2 %collective-permute-start.2 = (bf16[2,256,3,64]{1,3,2,0:T(8,128)(2,1)}, bf16[2,256,3,64]{1,3,2,0:T(8,128)(2,1)}, u32[]{:S(2)}, u32[]{:S(2)}) collective-permute-start(bf16[2,256,3,64]{1,3,2,0:T(8,128)(2,1)} %fusion.111), channel_id=1, source_target_pairs={{0,4},{4,8},{8,12},{12,16},{16,20},{20,24},{24,28},{28,0},{1,5},{5... | collective-permute-start | bytes 589832 | tf_op jit(solution)/shard_map/while/body/eval_jaxpr/ppermute | solution.py:13
  408.2 15.0 %collective-permute-start.3 = (bf16[2,256,3,64]{1,3,2,0:T(8,128)(2,1)}, bf16[2,256,3,64]{1,3,2,0:T(8,128)(2,1)S(1)}, u32[]{:S(2)}, u32[]{:S(2)}) collective-permute-start(bf16[2,256,3,64]{1,3,2,0:T(8,128)(2,1)} %fusion.112), channel_id=1, source_target_pairs={{0,4},{4,8},{8,12},{12,16},{16,20},{20,24},{24,28},{28,0},{1,5},{5... | collective-permute-start | bytes 589832 | tf_op jit(solution)/shard_map/while/body/eval_jaxpr/ppermute | solution.py:13
  424.1 21.4 %collective-permute-start = (bf16[2,256,3,64]{1,3,2,0:T(8,128)(2,1)S(1)}, bf16[2,256,3,64]{1,3,2,0:T(8,128)(2,1)S(1)}, u32[]{:S(2)}, u32[]{:S(2)}) collective-permute-start(bf16[2,256,3,64]{1,3,2,0:T(8,128)(2,1)S(1)} %copy.77), channel_id=1, source_target_pairs={{0,4},{4,8},{8,12},{12,16},{16,20},{20,24},{24,28},{28,0},{1,5},{5... | collective-permute-start | bytes 589832 | tf_op jit(solution)/shard_map/while/body/eval_jaxpr/ppermute | solution.py:13
  425.1 20.4 %collective-permute-start.1 = (bf16[2,256,3,64]{1,3,2,0:T(8,128)(2,1)S(1)}, bf16[2,256,3,64]{1,3,2,0:T(8,128)(2,1)}, u32[]{:S(2)}, u32[]{:S(2)}) collective-permute-start(bf16[2,256,3,64]{1,3,2,0:T(8,128)(2,1)S(1)} %copy.78), channel_id=1, source_target_pairs={{0,4},{4,8},{8,12},{12,16},{16,20},{20,24},{24,28},{28,0},{1,5},{5... | collective-permute-start | bytes 589832 | tf_op jit(solution)/shard_map/while/body/eval_jaxpr/ppermute | solution.py:13
  429.0 13.5 %collective-permute-start.2 = (bf16[2,256,3,64]{1,3,2,0:T(8,128)(2,1)}, bf16[2,256,3,64]{1,3,2,0:T(8,128)(2,1)}, u32[]{:S(2)}, u32[]{:S(2)}) collective-permute-start(bf16[2,256,3,64]{1,3,2,0:T(8,128)(2,1)} %fusion.111), channel_id=1, source_target_pairs={{0,4},{4,8},{8,12},{12,16},{16,20},{20,24},{24,28},{28,0},{1,5},{5... | collective-permute-start | bytes 589832 | tf_op jit(solution)/shard_map/while/body/eval_jaxpr/ppermute | solution.py:13
  431.3 13.4 %collective-permute-start.3 = (bf16[2,256,3,64]{1,3,2,0:T(8,128)(2,1)}, bf16[2,256,3,64]{1,3,2,0:T(8,128)(2,1)S(1)}, u32[]{:S(2)}, u32[]{:S(2)}) collective-permute-start(bf16[2,256,3,64]{1,3,2,0:T(8,128)(2,1)} %fusion.112), channel_id=1, source_target_pairs={{0,4},{4,8},{8,12},{12,16},{16,20},{20,24},{24,28},{28,0},{1,5},{5... | collective-permute-start | bytes 589832 | tf_op jit(solution)/shard_map/while/body/eval_jaxpr/ppermute | solution.py:13
  445.5 19.8 %collective-permute-start = (bf16[2,256,3,64]{1,3,2,0:T(8,128)(2,1)S(1)}, bf16[2,256,3,64]{1,3,2,0:T(8,128)(2,1)S(1)}, u32[]{:S(2)}, u32[]{:S(2)}) collective-permute-start(bf16[2,256,3,64]{1,3,2,0:T(8,128)(2,1)S(1)} %copy.77), channel_id=1, source_target_pairs={{0,4},{4,8},{8,12},{12,16},{16,20},{20,24},{24,28},{28,0},{1,5},{5... | collective-permute-start | bytes 589832 | tf_op jit(solution)/shard_map/while/body/eval_jaxpr/ppermute | solution.py:13
  446.5 18.8 %collective-permute-start.1 = (bf16[2,256,3,64]{1,3,2,0:T(8,128)(2,1)S(1)}, bf16[2,256,3,64]{1,3,2,0:T(8,128)(2,1)}, u32[]{:S(2)}, u32[]{:S(2)}) collective-permute-start(bf16[2,256,3,64]{1,3,2,0:T(8,128)(2,1)S(1)} %copy.78), channel_id=1, source_target_pairs={{0,4},{4,8},{8,12},{12,16},{16,20},{20,24},{24,28},{28,0},{1,5},{5... | collective-permute-start | bytes 589832 | tf_op jit(solution)/shard_map/while/body/eval_jaxpr/ppermute | solution.py:13
  450.5 12.0 %collective-permute-start.2 = (bf16[2,256,3,64]{1,3,2,0:T(8,128)(2,1)}, bf16[2,256,3,64]{1,3,2,0:T(8,128)(2,1)}, u32[]{:S(2)}, u32[]{:S(2)}) collective-permute-start(bf16[2,256,3,64]{1,3,2,0:T(8,128)(2,1)} %fusion.111), channel_id=1, source_target_pairs={{0,4},{4,8},{8,12},{12,16},{16,20},{20,24},{24,28},{28,0},{1,5},{5... | collective-permute-start | bytes 589832 | tf_op jit(solution)/shard_map/while/body/eval_jaxpr/ppermute | solution.py:13
  452.7 11.8 %collective-permute-start.3 = (bf16[2,256,3,64]{1,3,2,0:T(8,128)(2,1)}, bf16[2,256,3,64]{1,3,2,0:T(8,128)(2,1)S(1)}, u32[]{:S(2)}, u32[]{:S(2)}) collective-permute-start(bf16[2,256,3,64]{1,3,2,0:T(8,128)(2,1)} %fusion.112), channel_id=1, source_target_pairs={{0,4},{4,8},{8,12},{12,16},{16,20},{20,24},{24,28},{28,0},{1,5},{5... | collective-permute-start | bytes 589832 | tf_op jit(solution)/shard_map/while/body/eval_jaxpr/ppermute | solution.py:13
  465.3 19.8 %collective-permute-start = (bf16[2,256,3,64]{1,3,2,0:T(8,128)(2,1)S(1)}, bf16[2,256,3,64]{1,3,2,0:T(8,128)(2,1)S(1)}, u32[]{:S(2)}, u32[]{:S(2)}) collective-permute-start(bf16[2,256,3,64]{1,3,2,0:T(8,128)(2,1)S(1)} %copy.77), channel_id=1, source_target_pairs={{0,4},{4,8},{8,12},{12,16},{16,20},{20,24},{24,28},{28,0},{1,5},{5... | collective-permute-start | bytes 589832 | tf_op jit(solution)/shard_map/while/body/eval_jaxpr/ppermute | solution.py:13
  466.3 18.8 %collective-permute-start.1 = (bf16[2,256,3,64]{1,3,2,0:T(8,128)(2,1)S(1)}, bf16[2,256,3,64]{1,3,2,0:T(8,128)(2,1)}, u32[]{:S(2)}, u32[]{:S(2)}) collective-permute-start(bf16[2,256,3,64]{1,3,2,0:T(8,128)(2,1)S(1)} %copy.78), channel_id=1, source_target_pairs={{0,4},{4,8},{8,12},{12,16},{16,20},{20,24},{24,28},{28,0},{1,5},{5... | collective-permute-start | bytes 589832 | tf_op jit(solution)/shard_map/while/body/eval_jaxpr/ppermute | solution.py:13
  471.5 10.7 %collective-permute-start.2 = (bf16[2,256,3,64]{1,3,2,0:T(8,128)(2,1)}, bf16[2,256,3,64]{1,3,2,0:T(8,128)(2,1)}, u32[]{:S(2)}, u32[]{:S(2)}) collective-permute-start(bf16[2,256,3,64]{1,3,2,0:T(8,128)(2,1)} %fusion.111), channel_id=1, source_target_pairs={{0,4},{4,8},{8,12},{12,16},{16,20},{20,24},{24,28},{28,0},{1,5},{5... | collective-permute-start | bytes 589832 | tf_op jit(solution)/shard_map/while/body/eval_jaxpr/ppermute | solution.py:13
  473.8 10.4 %collective-permute-start.3 = (bf16[2,256,3,64]{1,3,2,0:T(8,128)(2,1)}, bf16[2,256,3,64]{1,3,2,0:T(8,128)(2,1)S(1)}, u32[]{:S(2)}, u32[]{:S(2)}) collective-permute-start(bf16[2,256,3,64]{1,3,2,0:T(8,128)(2,1)} %fusion.112), channel_id=1, source_target_pairs={{0,4},{4,8},{8,12},{12,16},{16,20},{20,24},{24,28},{28,0},{1,5},{5... | collective-permute-start | bytes 589832 | tf_op jit(solution)/shard_map/while/body/eval_jaxpr/ppermute | solution.py:13
  485.1 19.9 %collective-permute-start = (bf16[2,256,3,64]{1,3,2,0:T(8,128)(2,1)S(1)}, bf16[2,256,3,64]{1,3,2,0:T(8,128)(2,1)S(1)}, u32[]{:S(2)}, u32[]{:S(2)}) collective-permute-start(bf16[2,256,3,64]{1,3,2,0:T(8,128)(2,1)S(1)} %copy.77), channel_id=1, source_target_pairs={{0,4},{4,8},{8,12},{12,16},{16,20},{20,24},{24,28},{28,0},{1,5},{5... | collective-permute-start | bytes 589832 | tf_op jit(solution)/shard_map/while/body/eval_jaxpr/ppermute | solution.py:13
  486.1 18.9 %collective-permute-start.1 = (bf16[2,256,3,64]{1,3,2,0:T(8,128)(2,1)S(1)}, bf16[2,256,3,64]{1,3,2,0:T(8,128)(2,1)}, u32[]{:S(2)}, u32[]{:S(2)}) collective-permute-start(bf16[2,256,3,64]{1,3,2,0:T(8,128)(2,1)S(1)} %copy.78), channel_id=1, source_target_pairs={{0,4},{4,8},{8,12},{12,16},{16,20},{20,24},{24,28},{28,0},{1,5},{5... | collective-permute-start | bytes 589832 | tf_op jit(solution)/shard_map/while/body/eval_jaxpr/ppermute | solution.py:13
  493.3 8.8 %collective-permute-start.2 = (bf16[2,256,3,64]{1,3,2,0:T(8,128)(2,1)}, bf16[2,256,3,64]{1,3,2,0:T(8,128)(2,1)}, u32[]{:S(2)}, u32[]{:S(2)}) collective-permute-start(bf16[2,256,3,64]{1,3,2,0:T(8,128)(2,1)} %fusion.111), channel_id=1, source_target_pairs={{0,4},{4,8},{8,12},{12,16},{16,20},{20,24},{24,28},{28,0},{1,5},{5... | collective-permute-start | bytes 589832 | tf_op jit(solution)/shard_map/while/body/eval_jaxpr/ppermute | solution.py:13
  495.5 8.6 %collective-permute-start.3 = (bf16[2,256,3,64]{1,3,2,0:T(8,128)(2,1)}, bf16[2,256,3,64]{1,3,2,0:T(8,128)(2,1)S(1)}, u32[]{:S(2)}, u32[]{:S(2)}) collective-permute-start(bf16[2,256,3,64]{1,3,2,0:T(8,128)(2,1)} %fusion.112), channel_id=1, source_target_pairs={{0,4},{4,8},{8,12},{12,16},{16,20},{20,24},{24,28},{28,0},{1,5},{5... | collective-permute-start | bytes 589832 | tf_op jit(solution)/shard_map/while/body/eval_jaxpr/ppermute | solution.py:13
  505.0 28.4 %collective-permute-start = (bf16[2,256,3,64]{1,3,2,0:T(8,128)(2,1)S(1)}, bf16[2,256,3,64]{1,3,2,0:T(8,128)(2,1)S(1)}, u32[]{:S(2)}, u32[]{:S(2)}) collective-permute-start(bf16[2,256,3,64]{1,3,2,0:T(8,128)(2,1)S(1)} %copy.77), channel_id=1, source_target_pairs={{0,4},{4,8},{8,12},{12,16},{16,20},{20,24},{24,28},{28,0},{1,5},{5... | collective-permute-start | bytes 589832 | tf_op jit(solution)/shard_map/while/body/eval_jaxpr/ppermute | solution.py:13
  506.0 27.4 %collective-permute-start.1 = (bf16[2,256,3,64]{1,3,2,0:T(8,128)(2,1)S(1)}, bf16[2,256,3,64]{1,3,2,0:T(8,128)(2,1)}, u32[]{:S(2)}, u32[]{:S(2)}) collective-permute-start(bf16[2,256,3,64]{1,3,2,0:T(8,128)(2,1)S(1)} %copy.78), channel_id=1, source_target_pairs={{0,4},{4,8},{8,12},{12,16},{16,20},{20,24},{24,28},{28,0},{1,5},{5... | collective-permute-start | bytes 589832 | tf_op jit(solution)/shard_map/while/body/eval_jaxpr/ppermute | solution.py:13
  510.9 19.2 %collective-permute-start.2 = (bf16[2,256,3,64]{1,3,2,0:T(8,128)(2,1)}, bf16[2,256,3,64]{1,3,2,0:T(8,128)(2,1)}, u32[]{:S(2)}, u32[]{:S(2)}) collective-permute-start(bf16[2,256,3,64]{1,3,2,0:T(8,128)(2,1)} %fusion.111), channel_id=1, source_target_pairs={{0,4},{4,8},{8,12},{12,16},{16,20},{20,24},{24,28},{28,0},{1,5},{5... | collective-permute-start | bytes 589832 | tf_op jit(solution)/shard_map/while/body/eval_jaxpr/ppermute | solution.py:13
  513.2 19.4 %collective-permute-start.3 = (bf16[2,256,3,64]{1,3,2,0:T(8,128)(2,1)}, bf16[2,256,3,64]{1,3,2,0:T(8,128)(2,1)S(1)}, u32[]{:S(2)}, u32[]{:S(2)}) collective-permute-start(bf16[2,256,3,64]{1,3,2,0:T(8,128)(2,1)} %fusion.112), channel_id=1, source_target_pairs={{0,4},{4,8},{8,12},{12,16},{16,20},{20,24},{24,28},{28,0},{1,5},{5... | collective-permute-start | bytes 589832 | tf_op jit(solution)/shard_map/while/body/eval_jaxpr/ppermute | solution.py:13
  536.5 7.3 copy-start.3
  536.5 7.3 copy-start.16
  536.5 7.3 copy-start.23
  540.0 15.2 %all-to-all-start.3 = ((bf16[2,256,3,1,192]{4,0,3,2,1:T(2,128)(2,1)}), bf16[2,256,3,1,192]{4,0,3,2,1:T(2,128)(2,1)S(1)}, u32[]{:S(2)}, u32[]{:S(2)}) async-start(bf16[2,256,3,1,192]{4,0,3,2,1:T(2,128)(2,1)} %copy.48), calls=%async_computation.3 | async-start | bytes 1572864 | tf_op jit(solution)/shard_map/all_to_all | solution.py:212
  543.6 275.9 %reduce-scatter.7.cloned.1.call-start = ((), (), s32[]{:S(2)}) async-start(), calls=%async_computation.12 | async-start | bytes 7299072 | tf_op jit(solution)/shard_map/reduce_scatter | solution.py:222
  561.7 44.4 %copy-start.5 = (f32[128,768]{1,0:T(8,128)S(1)}, f32[128,768]{1,0:T(8,128)}, u32[]{:S(2)}) copy-start(f32[128,768]{1,0:T(8,128)} %copy-done.4) | copy-start | bytes 1179652
  (17 other events, 67.5 us)
Sparse Core Ops, SparseCore 0:
  10.9 62.8 all-gather.6
  94.0 50.6 all-gather.14
  147.7 56.6 all-gather.8
  207.1 58.9 all-gather.10
  268.8 54.4 all-gather.12
  331.1 112.0 reduce-scatter.8
  450.1 119.5 reduce-scatter.12
  576.9 117.9 reduce-scatter.10
  701.1 118.2 reduce-scatter.6
